TPU v7x, 256 devices: a whole 4x4x8 slice. The times are simulated.
256 devices in a mesh: layer: 16 (over z_hi, y, core), phi: 16 (over x, z_lo).
Axes of the slice: x: 4, y: 4, z: 8 (z_hi: 2, z_lo: 4; z = z_hi * 4 + z_lo), core: 2. Of those that a mesh axis runs over, the one named last changes fastest.
Arguments:
- features: bfloat16 [65536, 256], P(('layer', 'phi')), may hold values from -6 to 6
- w_layers: bfloat16 [4, 256, 256], replicated, may hold values from -0.375 to 0.375
- b_layers: float32 [4, 256], replicated, may hold values from -1.5 to 1.5
- w_coord: bfloat16 [16, 256], replicated, may hold values from -0.09375 to 0.09375
- w_beta: bfloat16 [256], replicated, may hold values from -0.375 to 0.375
- point_hit: int32 [2048], P(('layer', 'phi')), may hold values from 0 to 255
- track: int32 [65536], P(('layer', 'phi')), may hold values from 0 to 2047
- noise: int32 [65536], P(('layer', 'phi')), may hold values 0 or 1
Outputs:
- grad_w_layers: float32 [4, 256, 256], replicated
- grad_b_layers: float32 [4, 256], replicated
- grad_w_coord: float32 [16, 256], replicated
- grad_w_beta: float32 [256], replicated
- loss: float32 [], replicated
Inputs may be any that keep to these rules, and one draw needn't show every extreme that they name: `point_hit`: an index among the 256 hits of the device holding the entry. A non-noise hit of track k is attracted to point k.
All inputs are finite; a program needn't handle non-finite values. No bound on the sum of `noise` on one device may be relied on, other than what follows from the above.
Results may differ from a plain program's by a relative error of at most 0.0013.
Values sent between devices are 32-bit elements; how exact they have to be, the bound alone decides.
A program may use at most 64 MiB of HBM per device.

v0:
```python
import jax
import jax.numpy as jnp
from jax import lax
from jax.sharding import PartitionSpec as P

dist_eps = 0.0001
charge_floor = 0.5
block_cols = 512


def mlp_forward(features, w_layers, b_layers, w_coord, w_beta):
    hidden = features
    states = [features]
    preacts = []
    for layer_num in range(w_layers.shape[0]):
        pre = (
            jnp.dot(hidden, w_layers[layer_num], preferred_element_type=jnp.float32)
            + b_layers[layer_num]
        )
        preacts.append(pre)
        hidden = jax.nn.silu(pre).astype(jnp.bfloat16)
        states.append(hidden)
    coords = lax.dot_general(
        w_coord, hidden, (((1,), (1,)), ((), ())), preferred_element_type=jnp.float32
    )
    logits = jnp.dot(hidden, w_beta, preferred_element_type=jnp.float32)
    return (states, preacts, coords, logits)


def charges(logits):
    expz = jnp.exp(logits)
    spread = jnp.log1p(2.0 * expz)
    charge = 0.25 * spread * spread + charge_floor
    slope = 0.5 * spread * (2.0 * expz / (1.0 + 2.0 * expz))
    return (jax.nn.sigmoid(logits), charge, slope)


def pair_terms(coords, charge, track, live, point_rows, first, hits_all):
    point_y = point_rows[:-1]
    point_q = point_rows[-1]
    width = point_rows.shape[1]
    hit_sq = jnp.sum(coords * coords, 0)
    point_sq = jnp.sum(point_y * point_y, 0)
    cross = lax.dot_general(
        coords,
        point_y,
        (((0,), (0,)), ((), ())),
        precision=lax.Precision.HIGHEST,
        preferred_element_type=jnp.float32,
    )
    dist_sq = jnp.maximum(hit_sq[:, None] + point_sq[None, :] - 2.0 * cross, 0.0)
    dist = jnp.sqrt(dist_sq + dist_eps)
    index = first + lax.iota(jnp.int32, width)
    match = jnp.where((track[:, None] == index[None, :]) & (live[:, None] > 0), 1.0, 0.0)
    reach = jnp.maximum(1.0 - dist, 0.0)
    potential = match * dist_sq + (1.0 - match) * reach * reach
    pot_rows = jnp.sum(potential * point_q[None, :], 1)
    coef = (
        (charge / hits_all)[:, None]
        * point_q[None, :]
        * (2.0 * match - (1.0 - match) * 2.0 * reach / dist)
    )
    row_sums = jnp.sum(coef, 1)
    col_sums = jnp.sum(coef, 0)
    pulls = lax.dot_general(
        point_y,
        coef,
        (((1,), (1,)), ((), ())),
        precision=lax.Precision.HIGHEST,
        preferred_element_type=jnp.float32,
    )
    point_grad = point_y * col_sums[None, :] - lax.dot_general(
        coords,
        coef,
        (((1,), (0,)), ((), ())),
        precision=lax.Precision.HIGHEST,
        preferred_element_type=jnp.float32,
    )
    charge_grad = jnp.dot(charge, potential, precision=lax.Precision.HIGHEST) / hits_all
    return (row_sums, pot_rows, pulls, jnp.concatenate([point_grad, charge_grad[None, :]], 0))


def on_device(features, w_layers, b_layers, w_coord, w_beta, point_hit, track, noise):
    hit_count = features.shape[0]
    point_count = point_hit.shape[0]
    ndev = lax.axis_size("layer") * lax.axis_size("phi")
    total_points = point_count * ndev
    hits_all = hit_count * ndev * 1.0
    states, preacts, coords, logits = mlp_forward(features, w_layers, b_layers, w_coord, w_beta)
    beta_vals, charge, slope = charges(logits)
    selector = jnp.where(point_hit[:, None] == lax.iota(jnp.int32, hit_count)[None, :], 1.0, 0.0)
    own_y = lax.dot_general(
        coords,
        selector,
        (((1,), (1,)), ((), ())),
        precision=lax.Precision.HIGHEST,
        preferred_element_type=jnp.float32,
    )
    own_q = jnp.dot(selector, charge, precision=lax.Precision.HIGHEST)
    own_beta = jnp.dot(selector, beta_vals, precision=lax.Precision.HIGHEST)
    own_rows = jnp.concatenate([own_y, own_q[None, :]], 0)
    live = 1 - noise
    init = (
        jnp.zeros((hit_count,), jnp.float32),
        jnp.zeros((hit_count,), jnp.float32),
        jnp.zeros(coords.shape, jnp.float32),
        jnp.zeros((own_rows.shape[0], total_points), jnp.float32),
    )
    piece = lax.all_gather(own_rows, ("layer", "phi"), axis=1, tiled=True)
    width = piece.shape[1]

    def one_block(state, offset, cols):
        row_acc, pot_acc, pull_acc, grad_acc = state
        block = lax.dynamic_slice_in_dim(piece, offset, cols, 1)
        row_sums, pot_rows, pulls, point_grads = pair_terms(
            coords, charge, track, live, block, offset, hits_all
        )
        grad_acc = lax.dynamic_update_slice_in_dim(grad_acc, point_grads, offset, 1)
        return (row_acc + row_sums, pot_acc + pot_rows, pull_acc + pulls, grad_acc)

    full = width // block_cols
    state = init
    state = lax.fori_loop(
        0, full, lambda step, inner: one_block(inner, step * block_cols, block_cols), state
    )
    row_sums, pot_rows, pulls, point_grads = state
    own_grads = lax.psum_scatter(point_grads, ("layer", "phi"), scatter_dimension=1, tiled=True)
    coord_dim = coords.shape[0]
    coord_grad = coords * row_sums[None, :] - pulls
    coord_grad = coord_grad + jnp.dot(
        own_grads[:coord_dim], selector, precision=lax.Precision.HIGHEST
    )
    charge_grad = pot_rows / hits_all + jnp.dot(
        own_grads[coord_dim], selector, precision=lax.Precision.HIGHEST
    )
    noise_float = noise.astype(jnp.float32)
    beta_grad = noise_float / hits_all + jnp.sum(selector, 0) * (-1.0 / total_points)
    logit_grad = charge_grad * slope + beta_grad * beta_vals * (1.0 - beta_vals)
    loss_local = (
        jnp.sum(charge * pot_rows) / hits_all
        + jnp.sum(1.0 - own_beta) / total_points
        + jnp.sum(noise_float * beta_vals) / hits_all
    )
    coord_low = coord_grad.astype(jnp.bfloat16)
    logit_low = logit_grad.astype(jnp.bfloat16)
    hidden = states[-1]
    grad_coord_w = lax.dot_general(
        coord_low, hidden, (((1,), (0,)), ((), ())), preferred_element_type=jnp.float32
    )
    grad_beta_w = jnp.dot(logit_low, hidden, preferred_element_type=jnp.float32)
    upstream = lax.dot_general(
        coord_low, w_coord, (((0,), (0,)), ((), ())), preferred_element_type=jnp.float32
    )
    upstream = (
        upstream + logit_low.astype(jnp.float32)[:, None] * w_beta.astype(jnp.float32)[None, :]
    )
    count = w_layers.shape[0]
    weight_grads = [None] * count
    bias_grads = [None] * count
    for layer_num in range(count - 1, -1, -1):
        pre = preacts[layer_num]
        sig = jax.nn.sigmoid(pre)
        local = (upstream * sig * (1.0 + pre * (1.0 - sig))).astype(jnp.bfloat16)
        weight_grad = lax.dot_general(
            states[layer_num], local, (((0,), (0,)), ((), ())), preferred_element_type=jnp.float32
        )
        bias_grad = jnp.sum(local.astype(jnp.float32), 0)
        if layer_num > 0:
            upstream = lax.dot_general(
                local,
                w_layers[layer_num],
                (((1,), (1,)), ((), ())),
                preferred_element_type=jnp.float32,
            )
        weight_grads[layer_num] = weight_grad
        bias_grads[layer_num] = bias_grad
    grad_w_layers = jnp.stack(weight_grads)
    grad_b_layers = jnp.stack(bias_grads)
    grad_w_layers, grad_b_layers, grad_coord_w, grad_beta_w, loss_local = lax.psum(
        (grad_w_layers, grad_b_layers, grad_coord_w, grad_beta_w, loss_local), ("layer", "phi")
    )
    return (grad_w_layers, grad_b_layers, grad_coord_w, grad_beta_w, loss_local)


def solution(mesh):
    return jax.shard_map(
        on_device,
        mesh=mesh,
        in_specs=(
            P(("layer", "phi"), None),
            P(),
            P(),
            P(),
            P(),
            P(("layer", "phi")),
            P(("layer", "phi")),
            P(("layer", "phi")),
        ),
        out_specs=(P(), P(), P(), P(), P()),
        check_vma=False,
    )
```

profile of v0, /device:TPU:1, one launch (start us, length us, event | category | flops | bytes accessed | tf_op | source)
XLA Modules:
  0.0 1170.3 jit_solution(12711560222220822224)
XLA Ops:
  7.3 0.7 reshape.37
  8.0 0.7 broadcast_subtract_fusion
  8.7 0.8 fusion.82
  9.5 1.1 convolution_add_fusion.4
  11.5 0.7 copy-done.3
  13.0 0.6 copy-done.7
  14.1 604.9 %all_gather.3 = f32[17,2048]{0,1:T(8,128)S(1)} all-gather(f32[17,8]{0,1:T(8,128)S(1)} %pad_maximum_fusion.1), channel_id=1, replica_groups=mesh['layer'=16,'phi'=16] {'layer','phi'}, dimensions={1}, use_global_device_ids=true | all-gather | bytes 139808 | tf_op jit(solution)/shard_map/all_gather | solution.py:109
  619.4 0.7 copy-done.5
  620.1 11.6 while.22
  620.1 1.3 multiply_reduce_fusion.8
  623.1 1.3 multiply_reduce_fusion.8
  626.0 1.3 multiply_reduce_fusion.8
  628.9 1.3 multiply_reduce_fusion.8
  631.7 0.7 copy-done.1
  632.5 0.6 copy-done.6
  633.1 0.8 fusion.25
  635.3 265.8 %all-reduce.7.cloned.1.call-done = f32[17,2048]{1,0:T(8,128)} async-done(((f32[17,2048]{1,0:T(8,128)}), f32[17,2048]{1,0:T(8,128)}) %all-reduce.7.cloned.1.call-update) | async-done | bytes 139280
  901.1 0.9 fusion.41
  902.0 0.6 fusion.81
  902.6 0.9 fusion.23
  906.2 1.0 pad_maximum_fusion
  907.6 76.6 %all-reduce.1 = (f32[4,256]{1,0:T(4,128)}, f32[16,256]{1,0:T(8,128)}, f32[256]{0:T(256)}, f32[]{:T(128)}) all-reduce(f32[4,256]{1,0:T(4,128)S(1)} %pad_maximum_fusion.2, f32[16,256]{1,0:T(8,128)S(1)} %fusion.85, f32[256]{0:T(256)S(1)} %bitcast.138, f32[]{:T(128)S(6)} %add.271), channel_id=1, replica_groups=mesh['layer'=16,'phi'=16] {'layer','phi'}, use_global_device_ids=true, to_apply=%region_14.15 | all-reduce | flops 5377 | bytes 43016 | tf_op jit(solution)/shard_map/psum | solution.py:179
  984.2 176.7 %all-reduce.5.cloned.1.call-done = f32[4,256,256]{1,2,0:T(8,128)} async-done(((f32[4,256,256]{1,2,0:T(8,128)}), f32[4,256,256]{1,2,0:T(8,128)}) %all-reduce.5.cloned.1.call-update) | async-done | bytes 1048592 | tf_op jit(solution)/shard_map/psum | solution.py:179
  1160.9 2.5 copy.30
  (87 shorter events, 11.0 us)
Async XLA Ops:
  7.2 2.4 copy-start
  7.2 3.4 copy-start.2
  7.2 893.9 %all-reduce.7.cloned.1.call-start = ((), (), s32[]{:S(2)}) async-start(), calls=%async_computation.1 | async-start | bytes 393216
  11.3 1.5 copy-start.4
  11.5 0.7 copy-start.3
  13.0 0.7 copy-start.7
  619.4 0.7 copy-start.5
  631.7 0.7 copy-start.1
  632.4 528.5 %all-reduce.5.cloned.1.call-start = ((), (), s32[]{:S(2)}) async-start(), calls=%async_computation | async-start | bytes 2097152 | tf_op jit(solution)/shard_map/psum | solution.py:179
  632.4 0.7 copy-start.6
Sparse Core Ops, SparseCore 0:
  632.5 268.5 all-reduce.6
  907.4 253.4 all-reduce.4
where the time goes:
time: 1170 us
  blocking collectives  682 us (58%)
  waiting for transfers between devices  443 us (38%)
  matrix products  18.3 us (2%)
  between operations  16.2 us (1%)
    all_gather x1, blocking collectives, on_device(): piece = lax.all_gather(own_rows, ('layer', 'phi'), axis=1, tiled=True)  605 us
    unnamed x3, waiting for transfers between devices  266 us
    psum x1, waiting for transfers between devices, on_device(): lax.psum((grad_w_layers, grad_b_layers, grad_coord_w, grad_beta_w, loss_l...  177 us
    psum x1, blocking collectives, on_device(): lax.psum((grad_w_layers, grad_b_layers, grad_coord_w, grad_beta_w, loss_l...  76.6 us
  transfers between devices with their start and end apart: 2, of which 2 were waited for; matrix products, arithmetic and copies ran while one was open for 0% of the time, Pallas kernels for 0%

commit v1 on v0

v1 whole, which is shorter than its diff:
```python
import jax
import jax.numpy as jnp
from jax import lax
from jax.sharding import PartitionSpec as P
from jax.experimental import pallas as pl
from jax.experimental.pallas import tpu as pltpu

f32 = jnp.float32
bf16 = jnp.bfloat16
dist_eps = 0.0001
charge_floor = 0.5
MESH = pl.DeviceIdType.MESH
HITS = 65536.0
POINTS = 2048.0


def split3(v):
    hi = v.astype(bf16).astype(f32)
    rest = v - hi
    mid = rest.astype(bf16).astype(f32)
    low = (rest - mid).astype(bf16).astype(f32)
    return hi, mid, low


def rows_of(shape):
    return lax.broadcasted_iota(jnp.int32, shape, 0)


def lanes_of(shape):
    return lax.broadcasted_iota(jnp.int32, shape, 1)


def nt_dot(a, b):
    return lax.dot_general(a, b, (((1,), (1,)), ((), ())), preferred_element_type=f32)


def tn_dot(a, b):
    return lax.dot_general(a, b, (((0,), (0,)), ((), ())), preferred_element_type=f32)


def kernel(
    feat_ref, w_ref, b_ref, wc_ref, wb_ref, hit_ref, track_ref, noise_ref,
    gw_ref, gb_ref, gc_ref, gbeta_ref, loss_ref,
    pre_ref, act_ref, actt_ref,
    hits_ref, hits_back, hits_out, pts_ref, pts_back, pts_out,
    ycat_ref, yqt_ref, qp_ref, id_ref, pot_ref, ptacc_ref,
    part_ref, core_in, xy_in, zsum_ref, full_ref,
    s_hit, r_hit, s_pt, r_pt, s_hb, r_hb, s_pb, r_pb,
    s_core, r_core, s_xy, r_xy, s_z, r_z, s_g, r_g, s_f, r_f,
):
    lay = lax.axis_index("layer")
    phi = lax.axis_index("phi")
    z = (lay // 8) * 4 + phi % 4
    y = (lay // 2) % 4
    core = lay % 2
    x = phi // 4
    other = 1 - core
    here = x * 4 + y

    def device(px, py, pz, pc):
        return ((pz // 4) * 8 + py * 2 + pc, px * 4 + pz % 4)

    def plane(step):
        return device((x + step // 4) % 4, (y + step % 4) % 4, z, core)

    def plane_back(step):
        return device((x + 4 - step // 4) % 4, (y + 4 - step % 4) % 4, z, core)

    def column(step):
        return device(x, y, (z + step // 2) % 8, (core + step % 2) % 2)

    def column_back(step):
        return device(x, y, (z + 8 - step // 2) % 8, (core + 2 - step % 2) % 2)

    def ring(step):
        return device(x, y, (z + step) % 8, core)

    partner = device(x, y, z, other)

    def copy(src, dst, ssem, rsem, target):
        return pltpu.make_async_remote_copy(
            src_ref=src, dst_ref=dst, send_sem=ssem, recv_sem=rsem,
            device_id=target, device_id_type=MESH,
        )

    def each(first, last, body):
        def step(i, carry):
            body(i)
            return carry
        lax.fori_loop(first, last, step, 0)

    barrier = pltpu.get_barrier_semaphore()

    def greet(i):
        pl.semaphore_signal(barrier, inc=1, device_id=plane(i), device_id_type=MESH)
        pl.semaphore_signal(barrier, inc=1, device_id=column(i), device_id_type=MESH)
    each(1, 16, greet)

    hidden = feat_ref[...]
    for layer in range(4):
        pre = jnp.dot(hidden, w_ref[layer], preferred_element_type=f32) + b_ref[layer : layer + 1, :]
        pre_ref[layer] = pre
        hidden = (pre * jax.nn.sigmoid(pre)).astype(bf16)
        act_ref[layer] = hidden
    wcb = jnp.concatenate(
        [
            wc_ref[...].astype(f32),
            jnp.where(rows_of((16, 256)) == 0, wb_ref[...].astype(f32).reshape(1, 256), 0.0),
        ],
        0,
    ).astype(bf16)
    xz = nt_dot(wcb, hidden)
    coords = xz[0:16]
    logits = xz[16:17]
    expz = jnp.exp(logits)
    spread = jnp.log1p(2.0 * expz)
    charge = 0.25 * spread * spread + charge_floor
    slope = 0.5 * spread * (2.0 * expz / (1.0 + 2.0 * expz))
    beta = jax.nn.sigmoid(logits)
    noise = noise_ref[...].reshape(1, 256)
    track = track_ref[...].reshape(1, 256)
    key = jnp.where(noise == 0, track, -1).astype(f32)
    noise_f = noise.astype(f32)
    square = jnp.sum(coords * coords, 0, keepdims=True)
    row8 = rows_of((8, 256))
    lane8 = lanes_of((8, 256))
    pack = jnp.where(row8 == 0, charge, jnp.where(row8 == 1, key, jnp.where(row8 == 2, square, 0.0)))
    mine = jnp.concatenate([coords, pack], 0)
    hits_ref[0] = mine
    sel = jnp.zeros((8, 256), f32)
    for k in range(8):
        sel = jnp.where((row8 == k) & (lane8 == hit_ref[k]), 1.0, sel)
    sel_low = sel.astype(bf16)
    mine128 = jnp.concatenate([mine, jnp.zeros((104, 256), f32)], 0)
    mh, mm, ml = split3(mine128)
    own_pts = (nt_dot(sel_low, mh.astype(bf16)) + nt_dot(sel_low, mm.astype(bf16))) + nt_dot(sel_low, ml.astype(bf16))
    linear = lay * 16 + phi
    ident = (linear * 8 + rows_of((8, 128))).astype(f32)
    own_pts = jnp.where(lanes_of((8, 128)) == 17, ident, own_pts)
    pts_ref[0] = own_pts

    pl.semaphore_wait(barrier, 30)

    def pt_copy(i):
        return copy(pts_ref.at[0], pts_ref.at[i], s_pt.at[i], r_pt.at[i], column(i))

    def hit_copy(i):
        return copy(hits_ref.at[0], hits_ref.at[i], s_hit.at[i], r_hit.at[i], plane(i))

    each(1, 16, lambda i: pt_copy(i).start())
    each(1, 16, lambda i: hit_copy(i).start())

    actt_ref[0] = feat_ref[...].T
    for layer in range(4):
        pre = pre_ref[layer]
        sig = jax.nn.sigmoid(pre)
        pre_ref[layer] = sig * (1.0 + pre * (1.0 - sig))
        if layer < 3:
            actt_ref[layer + 1] = act_ref[layer].T
    ptacc_ref[...] = jnp.zeros((128, 128), f32)
    pot_ref[...] = jnp.zeros((128, 256), f32)

    each(1, 16, lambda i: pt_copy(i).wait())
    points = pts_ref[...].reshape(128, 128)
    qp_ref[...] = jnp.broadcast_to(points[:, 16:17], (128, 256))
    id_ref[...] = jnp.broadcast_to(points[:, 17:18], (128, 256))
    pt = points.T
    y_t = pt[0:16]
    qp_t = pt[16:17]
    yh, ym, yl = split3(-2.0 * y_t)
    sqh, sqm, sql = split3(pt[18:19])
    row16 = rows_of((16, 128))
    tail = jnp.where(row16 < 3, 1.0, jnp.where(row16 == 3, sqh, jnp.where(row16 == 4, sqm, jnp.where(row16 == 5, sql, 0.0))))
    ycat_ref[...] = jnp.concatenate([yh, yh, ym, ym, yh, yl, tail, jnp.zeros((16, 128), f32)], 0).T.astype(bf16)
    yq = jnp.concatenate([y_t * qp_t, jnp.where(row16 == 0, qp_t, 0.0)], 0)
    yqh, yqm, yql = split3(yq)
    yqt = jnp.concatenate([yqh, yqm, yql], 0).astype(bf16)
    yqt_ref[...] = jnp.concatenate([yqt, yqt], 1)

    def hb_copy(i):
        return copy(hits_out.at[i], hits_back.at[i], s_hb.at[i], r_hb.at[i], plane_back(i))

    def pairs(i):
        @pl.when(i > 0)
        def _():
            hit_copy(i).wait()

        blk = hits_ref[i]
        xs = blk[0:16]
        q = blk[16:17]
        key_i = blk[17:18]
        xh, xm, xl = split3(xs)
        sh, sm, sl = split3(blk[18:19])
        r16 = rows_of((16, 256))
        tail_x = jnp.where(r16 == 0, sh, jnp.where(r16 == 1, sm, jnp.where(r16 == 2, sl, jnp.where(r16 < 6, 1.0, 0.0))))
        xcat = jnp.concatenate([xh, xm, xh, xm, xl, xh, tail_x, jnp.zeros((16, 256), f32)], 0).astype(bf16)
        d2 = jnp.maximum(jnp.dot(ycat_ref[...], xcat, preferred_element_type=f32), 0.0)
        t = d2 + dist_eps
        inv = lax.rsqrt(t)
        reach = jnp.maximum(1.0 - t * inv, 0.0)
        match = id_ref[...] == key_i
        pot = jnp.where(match, d2, reach * reach)
        cc = jnp.where(match, 1.0, -(reach * inv))
        pot_rows = jnp.sum(pot * qp_ref[...], 0, keepdims=True)
        pot_ref[...] += pot * q
        cc_hi = cc.astype(bf16)
        cc_lo = (cc - cc_hi.astype(f32)).astype(bf16)
        ht = jnp.dot(yqt_ref[...], jnp.concatenate([cc_hi, cc_lo], 0), preferred_element_type=f32)
        ht = (ht[0:32] + ht[32:64]) + ht[64:96]
        hits_out[i] = jnp.concatenate([ht[0:16], jnp.where(row8 == 1, pot_rows, ht[16:24])], 0)
        xq = jnp.concatenate([xs * q, jnp.where(r16 == 0, q, 0.0)], 0)
        xqh, xqm, xql = split3(xq)
        xq_all = jnp.concatenate([xqh, xqm, xql, jnp.zeros((32, 256), f32)], 0).astype(bf16)
        ptacc_ref[...] += nt_dot(cc_hi, xq_all) + nt_dot(cc_lo, xq_all)

        @pl.when(i > 0)
        def _():
            hb_copy(i).start()

    each(0, 16, pairs)

    acc = ptacc_ref[...]
    acc = (acc + pltpu.roll(acc, 96, 1)) + pltpu.roll(acc, 64, 1)
    pot_cols = jnp.sum(pot_ref[...], 1, keepdims=True)
    pts_out[...] = jnp.where(lanes_of((128, 128)) == 17, pot_cols, acc).reshape(16, 8, 128)

    def pb_copy(i):
        return copy(pts_out.at[i], pts_back.at[i], s_pb.at[i], r_pb.at[i], column_back(i))

    each(1, 16, lambda i: pb_copy(i).start())
    each(1, 16, lambda i: hb_copy(i).wait())
    hsum = hits_out[0]
    for i in range(1, 16):
        hsum = hsum + hits_back[i]
    pot_i = hsum[17:18]
    coord_grad = (2.0 * charge / HITS) * (coords * hsum[16:17] - hsum[0:16])
    each(1, 16, lambda i: pb_copy(i).wait())
    psum = pts_out[0]
    for i in range(1, 16):
        psum = psum + pts_back[i]
    lane = lanes_of((8, 128))
    grads = jnp.where(
        lane < 16,
        (2.0 * own_pts[:, 16:17] / HITS) * (own_pts * psum[:, 16:17] - psum),
        jnp.where(lane == 16, psum[:, 17:18] / HITS, 0.0),
    )
    gh, gm, gl = split3(grads)
    zeros8 = jnp.zeros((8, 128), f32)
    g3 = jnp.concatenate([gh, gm, gl, zeros8], 0).astype(bf16)
    sel3 = jnp.concatenate([sel, sel, sel, jnp.zeros((8, 256), f32)], 0).astype(bf16)
    spread_back = tn_dot(g3, sel3)
    count = jnp.sum(sel, 0, keepdims=True)
    coord_grad = coord_grad + spread_back[0:16]
    charge_grad = pot_i / HITS + spread_back[16:17]
    beta_grad = noise_f / HITS - count * (1.0 / POINTS)
    logit_grad = charge_grad * slope + beta_grad * beta * (1.0 - beta)
    loss_row = charge * pot_i / HITS + (count - count * beta) / POINTS + noise_f * beta / HITS
    loss_local = jnp.sum(loss_row, 1, keepdims=True)

    low = jnp.concatenate([coord_grad, jnp.where(rows_of((16, 256)) == 0, logit_grad, 0.0)], 0).astype(bf16)
    head = jnp.dot(low, act_ref[3], preferred_element_type=f32)
    up = tn_dot(low, wcb)

    def core_copy(j):
        if j < 4:
            src = part_ref.at[other, :, pl.ds(2 * j, 2)]
            dst = core_in.at[:, pl.ds(2 * j, 2)]
        else:
            src = part_ref.at[other, :, pl.ds(8, 1)]
            dst = core_in.at[:, pl.ds(8, 1)]
        return copy(src, dst, s_core.at[j], r_core.at[j], partner)

    biases = [None] * 4
    for layer in range(3, -1, -1):
        local = (up * pre_ref[layer]).astype(bf16)
        wg = jnp.dot(actt_ref[layer], local, preferred_element_type=f32)
        for half in range(2):
            part_ref[:, :, 2 * layer + half] = wg[:, half * 128 : half * 128 + 128].reshape(2, 16, 8, 128)
        core_copy(layer).start()
        biases[layer] = jnp.sum(local.astype(f32), 0, keepdims=True)
        if layer > 0:
            up = nt_dot(local, w_ref[layer])
    ext8 = jnp.where(
        row8 == 0,
        head[16:17],
        jnp.where(
            row8 == 1,
            biases[0],
            jnp.where(
                row8 == 2,
                biases[1],
                jnp.where(row8 == 3, biases[2], jnp.where(row8 == 4, biases[3], jnp.where(row8 == 5, loss_local, 0.0))),
            ),
        ),
    )
    ext = jnp.concatenate([head[0:16], ext8], 0)
    for half in range(2):
        cols = ext[:, half * 128 : half * 128 + 128].reshape(3, 8, 128)
        part_ref[half, :, 8] = jnp.concatenate([cols, jnp.zeros((13, 8, 128), f32)], 0)
    core_copy(4).start()
    for j in (3, 2, 1, 0, 4):
        core_copy(j).wait()
    part_ref[core] = part_ref[core] + core_in[...]

    def xy_copy(i):
        target = ((x + i // 4) % 4) * 4 + (y + i % 4) % 4
        return copy(part_ref.at[core, target], xy_in.at[i], s_xy.at[i], r_xy.at[i], plane(i))

    each(1, 16, lambda i: xy_copy(i).start())
    each(1, 16, lambda i: xy_copy(i).wait())
    total = part_ref[core, here]
    for i in range(1, 16):
        total = total + xy_in[i]
    zsum_ref[z] = total

    def z_copy(i):
        return copy(zsum_ref.at[z], zsum_ref.at[z], s_z.at[i], r_z.at[i], ring(i))

    each(1, 8, lambda i: z_copy(i).start())
    each(1, 8, lambda i: z_copy(i).wait())
    total = zsum_ref[0]
    for i in range(1, 8):
        total = total + zsum_ref[i]
    full_ref[core, here] = total

    def g_copy(i):
        return copy(full_ref.at[core, here], full_ref.at[core, here], s_g.at[i], r_g.at[i], plane(i))

    def f_copy(i):
        block = ((x + 4 - i // 4) % 4) * 4 + (y + 4 - i % 4) % 4
        return copy(full_ref.at[core, block], full_ref.at[core, block], s_f.at[i], r_f.at[i], partner)

    each(1, 16, lambda i: g_copy(i).start())
    f_copy(0).start()

    def forward_on(i):
        g_copy(i).wait_recv()
        f_copy(i).start()

    each(1, 16, forward_on)
    each(1, 16, lambda i: g_copy(i).wait_send())
    each(0, 16, lambda i: f_copy(i).wait())
    for layer in range(4):
        for half in range(2):
            gw_ref[layer, :, half * 128 : half * 128 + 128] = full_ref[:, :, 2 * layer + half].reshape(256, 128)
    gc_ref[...] = jnp.concatenate(
        [full_ref[half, 0:2, 8].reshape(16, 128) for half in range(2)], 1
    )
    last = jnp.concatenate([full_ref[half, 2, 8] for half in range(2)], 1)
    gbeta_ref[...] = last[0:1]
    gb_ref[...] = last[1:5]
    loss_ref[...] = last[5:6, 0:128]


def on_device(features, w_layers, b_layers, w_coord, w_beta, point_hit, track, noise):
    vmem = pl.BlockSpec(memory_space=pltpu.VMEM)
    smem = pl.BlockSpec(memory_space=pltpu.SMEM)
    dma = pltpu.SemaphoreType.DMA
    grad_w, grad_b, grad_c, grad_beta, loss = pl.pallas_call(
        kernel,
        name="condense",
        out_shape=(
            jax.ShapeDtypeStruct((4, 256, 256), f32),
            jax.ShapeDtypeStruct((4, 256), f32),
            jax.ShapeDtypeStruct((16, 256), f32),
            jax.ShapeDtypeStruct((1, 256), f32),
            jax.ShapeDtypeStruct((1, 128), f32),
        ),
        in_specs=[vmem] * 5 + [smem] + [vmem] * 2,
        out_specs=(vmem,) * 5,
        scratch_shapes=[
            pltpu.VMEM((4, 256, 256), f32),
            pltpu.VMEM((4, 256, 256), bf16),
            pltpu.VMEM((4, 256, 256), bf16),
            pltpu.VMEM((16, 24, 256), f32),
            pltpu.VMEM((16, 24, 256), f32),
            pltpu.VMEM((16, 24, 256), f32),
            pltpu.VMEM((16, 8, 128), f32),
            pltpu.VMEM((16, 8, 128), f32),
            pltpu.VMEM((16, 8, 128), f32),
            pltpu.VMEM((128, 128), bf16),
            pltpu.VMEM((96, 256), bf16),
            pltpu.VMEM((128, 256), f32),
            pltpu.VMEM((128, 256), f32),
            pltpu.VMEM((128, 256), f32),
            pltpu.VMEM((128, 128), f32),
            pltpu.VMEM((2, 16, 9, 8, 128), f32),
            pltpu.VMEM((16, 9, 8, 128), f32),
            pltpu.VMEM((16, 9, 8, 128), f32),
            pltpu.VMEM((8, 9, 8, 128), f32),
            pltpu.VMEM((2, 16, 9, 8, 128), f32),
            dma((16,)), dma((16,)), dma((16,)), dma((16,)),
            dma((16,)), dma((16,)), dma((16,)), dma((16,)),
            dma((5,)), dma((5,)), dma((16,)), dma((16,)),
            dma((8,)), dma((8,)), dma((16,)), dma((16,)),
            dma((16,)), dma((16,)),
        ],
        compiler_params=pltpu.CompilerParams(
            collective_id=0, has_side_effects=True, vmem_limit_bytes=48 << 20
        ),
    )(features, w_layers, b_layers, w_coord, w_beta, point_hit, track, noise)
    return grad_w, grad_b, grad_c, grad_beta.reshape(256), loss[0, 0]


def solution(mesh):
    return jax.shard_map(
        on_device,
        mesh=mesh,
        in_specs=(
            P(("layer", "phi"), None),
            P(),
            P(),
            P(),
            P(),
            P(("layer", "phi")),
            P(("layer", "phi")),
            P(("layer", "phi")),
        ),
        out_specs=(P(), P(), P(), P(), P()),
        check_vma=False,
    )
```

time: 1170 us -> 76.6 us (0.07)
  blocking collectives: 682 us -> 0 us
  waiting for transfers between devices: 443 us -> 0 us
  Pallas kernels: 0 us -> 65.8 us
  matrix products: 18.3 us -> 0 us
  between operations: 16.2 us -> 1.82 us
    all_gather x1 -> x0, blocking collectives: 605 us -> none  [on_device(): piece = lax.all_gather(own_rows, ('layer', 'phi'), axis=1, tiled=True)]
    unnamed x3 -> x0, waiting for transfers between devices: 266 us -> none
    psum x1 -> x0, waiting for transfers between devices: 177 us -> none  [on_device(): lax.psum((grad_w_layers, grad_b_layers, grad_coord_w, grad_beta_w, loss_l...]
    psum x1 -> x0, blocking collectives: 76.6 us -> none  [on_device(): lax.psum((grad_w_layers, grad_b_layers, grad_coord_w, grad_beta_w, loss_l...]
    pallas_call x0 -> x1, Pallas kernels: none -> 65.8 us  [on_device(): pl.pallas_call(kernel, name='condense', out_shape=(jax.ShapeDtypeStruct((...]
    dot_general x36 -> x0, matrix products: 18.1 us -> none  [the longest x4 5.27 us: pair_terms(): lax.dot_general(coords, point_y, (((0,), (0,)), ((), ())), precision=lax....]
  transfers between devices with their start and end apart: 2 -> 0, of which waited for: 2 -> 0; matrix products, arithmetic and copies ran while one was open for 0% -> 0% of each run, Pallas kernels for 0% -> 0%
where the time goes in v1:
time: 76.6 us; the launch traced here: 76.3 us
  Pallas kernels  65.8 us (86%)
  local copies, waits for them, and re-layouts  8.72 us (11%)
  between operations  1.82 us (2%)
    pallas_call x1, Pallas kernels, on_device(): pl.pallas_call(kernel, name='condense', out_shape=(jax.ShapeDtypeStruct((...  65.8 us
    unnamed x20, local copies, waits for them, and re-layouts  8.72 us

profile of v1, /device:TPU:1, one launch (start us, length us, event | category | flops | bytes accessed | tf_op | source)
XLA Modules:
  0.0 76.3 jit_solution(4178060836702663645)
XLA Ops:
  0.6 0.0 copy-start
  0.6 1.0 %copy-done = bf16[4,256,256]{2,1,0:T(8,128)(2,1)S(1)} copy-done((bf16[4,256,256]{2,1,0:T(8,128)(2,1)S(1)}, bf16[4,256,256]{2,1,0:T(8,128)(2,1)}, u32[]{:S(2)}) %copy-start) | copy-done | bytes 524312
  1.7 0.0 copy-start.1
  1.7 0.9 %copy-done.1 = bf16[256,256]{1,0:T(8,128)(2,1)S(1)} copy-done((bf16[256,256]{1,0:T(8,128)(2,1)S(1)}, bf16[256,256]{1,0:T(8,128)(2,1)}, u32[]{:S(2)}) %copy-start.1) | copy-done | bytes 131096
  2.6 0.0 copy-start.2
  2.6 0.7 copy-done.2
  3.3 0.0 copy-start.3
  3.3 0.7 copy-done.3
  4.0 0.0 copy-start.4
  4.0 0.7 copy-done.4
  4.6 0.0 copy-start.5
  4.6 0.7 copy-done.5
  5.3 0.0 copy-start.6
  5.3 0.7 copy-done.6
  6.0 0.0 copy-start.7
  6.0 0.7 copy-done.7
  6.6 65.8 %condense.1 = (f32[4,256,256]{2,1,0:T(8,128)S(1)}, f32[4,256]{1,0:T(4,128)S(1)}, f32[16,256]{1,0:T(8,128)S(1)}, f32[1,256]{1,0:T(1,128)S(1)}, f32[1,128]{1,0:T(1,128)S(1)}) custom-call(bf16[256,256]{1,0:T(8,128)(2,1)S(1)} %copy-done.1, bf16[4,256,256]{2,1,0:T(8,128)(2,1)S(1)} %copy-done, f32[4,256]{1,0:T(4,128)S(1)} %copy-done.3, ...), custom_call_target="tpu_custom_call" | custom-call | tf_op jit(solution)/shard_map/condense/pallas_call | solution.py:359
  72.4 1.0 %copy.18 = f32[4,256,256]{2,1,0:T(8,128)} copy(f32[4,256,256]{2,1,0:T(8,128)S(1)} %get-tuple-element.20) | data formatting | bytes 2097152
  73.4 0.6 copy.19
  74.0 0.6 copy.20
  74.6 0.6 copy.21
Async XLA Ops:
  0.6 1.0 %copy-start = (bf16[4,256,256]{2,1,0:T(8,128)(2,1)S(1)}, bf16[4,256,256]{2,1,0:T(8,128)(2,1)}, u32[]{:S(2)}) copy-start(bf16[4,256,256]{2,1,0:T(8,128)(2,1)} %w_ref.1) | copy-start | bytes 1572868
  1.7 0.9 %copy-start.1 = (bf16[256,256]{1,0:T(8,128)(2,1)S(1)}, bf16[256,256]{1,0:T(8,128)(2,1)}, u32[]{:S(2)}) copy-start(bf16[256,256]{1,0:T(8,128)(2,1)} %feat_ref.1) | copy-start | bytes 393220
  2.6 0.7 copy-start.2
  3.3 0.7 copy-start.3
  4.0 0.7 copy-start.4
  4.6 0.7 copy-start.5
  5.3 0.7 copy-start.6
  6.0 0.7 copy-start.7

commit v2 on v1

--- a/solution.py
+++ b/solution.py
@@ -39,8 +39,9 @@
 
 
 def kernel(
-    feat_ref, w_ref, b_ref, wc_ref, wb_ref, hit_ref, track_ref, noise_ref,
+    feat_hbm, w_hbm, b_hbm, wc_hbm, wb_hbm, hit_hbm, track_hbm, noise_hbm,
     gw_ref, gb_ref, gc_ref, gbeta_ref, loss_ref,
+    feat_ref, w_ref, b_ref, wc_ref, wb_ref, hit_ref, track_ref, noise_ref, s_in,
     pre_ref, act_ref, actt_ref,
     hits_ref, hits_back, hits_out, pts_ref, pts_back, pts_out,
     ycat_ref, yqt_ref, qp_ref, id_ref, pot_ref, ptacc_ref,
@@ -48,6 +49,26 @@
     s_hit, r_hit, s_pt, r_pt, s_hb, r_hb, s_pb, r_pb,
     s_core, r_core, s_xy, r_xy, s_z, r_z, s_g, r_g, s_f, r_f,
 ):
+    loads = [
+        pltpu.make_async_copy(src, dst, s_in.at[i])
+        for i, (src, dst) in enumerate(
+            [
+                (feat_hbm, feat_ref),
+                (w_hbm.at[0], w_ref.at[0]),
+                (b_hbm, b_ref),
+                (w_hbm.at[1], w_ref.at[1]),
+                (w_hbm.at[2], w_ref.at[2]),
+                (w_hbm.at[3], w_ref.at[3]),
+                (wc_hbm, wc_ref),
+                (wb_hbm, wb_ref),
+                (track_hbm, track_ref),
+                (noise_hbm, noise_ref),
+                (hit_hbm, hit_ref),
+            ]
+        )
+    ]
+    for load in loads:
+        load.start()
     lay = lax.axis_index("layer")
     phi = lax.axis_index("phi")
     z = (lay // 8) * 4 + phi % 4
@@ -96,12 +117,18 @@
         pl.semaphore_signal(barrier, inc=1, device_id=column(i), device_id_type=MESH)
     each(1, 16, greet)
 
+    for load in loads[0:3]:
+        load.wait()
     hidden = feat_ref[...]
     for layer in range(4):
+        if layer > 0:
+            loads[2 + layer].wait()
         pre = jnp.dot(hidden, w_ref[layer], preferred_element_type=f32) + b_ref[layer : layer + 1, :]
         pre_ref[layer] = pre
         hidden = (pre * jax.nn.sigmoid(pre)).astype(bf16)
         act_ref[layer] = hidden
+    for load in loads[6:11]:
+        load.wait()
     wcb = jnp.concatenate(
         [
             wc_ref[...].astype(f32),
@@ -349,26 +376,45 @@
     last = jnp.concatenate([full_ref[half, 2, 8] for half in range(2)], 1)
     gbeta_ref[...] = last[0:1]
     gb_ref[...] = last[1:5]
-    loss_ref[...] = last[5:6, 0:128]
+    loss_ref[...] = last[5:6, 0:1]
+
+
+def deliver(*refs):
+    sems = refs[10]
+    copies = [pltpu.make_async_copy(refs[i], refs[5 + i], sems.at[i]) for i in range(5)]
+    for copy in copies:
+        copy.start()
+    for copy in copies:
+        copy.wait()
 
 
 def on_device(features, w_layers, b_layers, w_coord, w_beta, point_hit, track, noise):
     vmem = pl.BlockSpec(memory_space=pltpu.VMEM)
-    smem = pl.BlockSpec(memory_space=pltpu.SMEM)
+    hbm = pl.BlockSpec(memory_space=pltpu.HBM)
     dma = pltpu.SemaphoreType.DMA
-    grad_w, grad_b, grad_c, grad_beta, loss = pl.pallas_call(
+    results = (
+        jax.ShapeDtypeStruct((4, 256, 256), f32),
+        jax.ShapeDtypeStruct((4, 256), f32),
+        jax.ShapeDtypeStruct((16, 256), f32),
+        jax.ShapeDtypeStruct((1, 256), f32),
+        jax.ShapeDtypeStruct((1, 1), f32),
+    )
+    grads = pl.pallas_call(
         kernel,
         name="condense",
-        out_shape=(
-            jax.ShapeDtypeStruct((4, 256, 256), f32),
-            jax.ShapeDtypeStruct((4, 256), f32),
-            jax.ShapeDtypeStruct((16, 256), f32),
-            jax.ShapeDtypeStruct((1, 256), f32),
-            jax.ShapeDtypeStruct((1, 128), f32),
-        ),
-        in_specs=[vmem] * 5 + [smem] + [vmem] * 2,
+        out_shape=results,
+        in_specs=[hbm] * 8,
         out_specs=(vmem,) * 5,
         scratch_shapes=[
+            pltpu.VMEM((256, 256), bf16),
+            pltpu.VMEM((4, 256, 256), bf16),
+            pltpu.VMEM((4, 256), f32),
+            pltpu.VMEM((16, 256), bf16),
+            pltpu.VMEM((256,), bf16),
+            pltpu.SMEM((8,), jnp.int32),
+            pltpu.VMEM((256,), jnp.int32),
+            pltpu.VMEM((256,), jnp.int32),
+            dma((11,)),
             pltpu.VMEM((4, 256, 256), f32),
             pltpu.VMEM((4, 256, 256), bf16),
             pltpu.VMEM((4, 256, 256), bf16),
@@ -398,8 +444,17 @@
         compiler_params=pltpu.CompilerParams(
             collective_id=0, has_side_effects=True, vmem_limit_bytes=48 << 20
         ),
-    )(features, w_layers, b_layers, w_coord, w_beta, point_hit, track, noise)
-    return grad_w, grad_b, grad_c, grad_beta.reshape(256), loss[0, 0]
+    )(*[pltpu.with_memory_space_constraint(v, pltpu.HBM) for v in (features, w_layers, b_layers, w_coord, w_beta, point_hit, track, noise)])
+    grad_w, grad_b, grad_c, grad_beta, loss = pl.pallas_call(
+        deliver,
+        name="deliver",
+        out_shape=results,
+        in_specs=[vmem] * 5,
+        out_specs=(hbm,) * 5,
+        scratch_shapes=[dma((5,))],
+        compiler_params=pltpu.CompilerParams(vmem_limit_bytes=8 << 20),
+    )(*grads)
+    return grad_w, grad_b, grad_c, grad_beta.reshape(256), loss.reshape(())
 
 
 def solution(mesh):

time: 76.6 us -> 67.9 us (0.89)
  local copies, waits for them, and re-layouts: 8.72 us -> 0 us
  Pallas kernels: 65.8 us -> 67.2 us
  between operations: 1.82 us -> 0.64 us
    unnamed x20 -> x0, local copies, waits for them, and re-layouts: 8.72 us -> none
    pallas_call x1 -> x2, Pallas kernels: 65.8 us -> 67.2 us  [the longest x1 65.5 us: on_device(): pl.pallas_call(kernel, name='condense', out_shape=results, in_specs=[hbm]...]
where the time goes in v2:
time: 67.9 us; the launch traced here: 67.8 us
  Pallas kernels  67.2 us (99%)
    pallas_call x1, Pallas kernels, on_device(): pl.pallas_call(kernel, name='condense', out_shape=results, in_specs=[hbm]...  65.5 us
    pallas_call x1, Pallas kernels, on_device(): pl.pallas_call(deliver, name='deliver', out_shape=results, in_specs=[vmem...  1.65 us

profile of v2, /device:TPU:1, one launch (start us, length us, event | category | flops | bytes accessed | tf_op | source)
XLA Modules:
  0.0 67.8 jit_solution(9767868181123707374)
XLA Ops:
  0.6 65.5 %condense.1 = (f32[4,256,256]{2,1,0:T(8,128)S(1)}, f32[4,256]{1,0:T(4,128)S(1)}, f32[16,256]{1,0:T(8,128)S(1)}, f32[1,256]{1,0:T(1,128)S(1)}, f32[1,1]{1,0:T(1,128)}) custom-call(bf16[256,256]{1,0:T(8,128)(2,1)} %feat_hbm.1, bf16[4,256,256]{2,1,0:T(8,128)(2,1)} %w_hbm.1, f32[4,256]{1,0:T(4,128)} %b_hbm.1, bf16[16,256]{1,0:T(8,128)(2,1)} %wc_hbm.1, ...), custom_call_target="tpu_custom_call" | custom-call | tf_op jit(solution)/shard_map/condense/pallas_call | solution.py:402
  66.2 1.7 %deliver.1 = (f32[4,256,256]{2,1,0:T(8,128)}, f32[4,256]{1,0:T(4,128)}, f32[16,256]{1,0:T(8,128)}, f32[1,256]{1,0:T(1,128)}, f32[1,1]{1,0:T(1,128)}) custom-call(f32[4,256,256]{2,1,0:T(8,128)S(1)} %get-tuple-element.15.refs_0_, f32[4,256]{1,0:T(4,128)S(1)} %get-tuple-element.16.refs_1_, f32[16,256]{1,0:T(8,128)S(1)} %get-tuple-element.17.refs_2_, ...), custom_call_target="tpu_custom_call" | custom-call | tf_op jit(solution)/shard_map/deliver/pallas_call | solution.py:448

commit v3 on v2

--- a/solution.py
+++ b/solution.py
@@ -12,6 +12,7 @@
 MESH = pl.DeviceIdType.MESH
 HITS = 65536.0
 POINTS = 2048.0
+chunks = ((0, 4), (4, 9))
 
 
 def split3(v):
@@ -289,24 +290,61 @@
     up = tn_dot(low, wcb)
 
     def core_copy(j):
-        if j < 4:
-            src = part_ref.at[other, :, pl.ds(2 * j, 2)]
-            dst = core_in.at[:, pl.ds(2 * j, 2)]
-        else:
-            src = part_ref.at[other, :, pl.ds(8, 1)]
-            dst = core_in.at[:, pl.ds(8, 1)]
-        return copy(src, dst, s_core.at[j], r_core.at[j], partner)
+        first, count = (2 * j, 2) if j < 4 else (8, 1)
+        return copy(
+            part_ref.at[other, :, pl.ds(first, count)], core_in.at[:, pl.ds(first, count)],
+            s_core.at[j], r_core.at[j], partner,
+        )
+
+    def core_sum(j):
+        core_copy(j).wait()
+        first, count = (2 * j, 2) if j < 4 else (8, 1)
+        part_ref[core, :, first : first + count] += core_in[:, first : first + count]
+
+    def xy_copy(c, i):
+        first, last = chunks[c]
+        span = pl.ds(first, last - first)
+        target = ((x + i // 4) % 4) * 4 + (y + i % 4) % 4
+        return copy(
+            part_ref.at[core, target, span], xy_in.at[i, span], s_xy.at[c, i], r_xy.at[c, i], plane(i)
+        )
+
+    def z_copy(c, i):
+        first, last = chunks[c]
+        span = pl.ds(first, last - first)
+        return copy(zsum_ref.at[z, span], zsum_ref.at[z, span], s_z.at[c, i], r_z.at[c, i], ring(i))
+
+    def g_copy(c, i):
+        first, last = chunks[c]
+        span = pl.ds(first, last - first)
+        block = full_ref.at[core, here, span]
+        return copy(block, block, s_g.at[c, i], r_g.at[c, i], plane(i))
+
+    def f_copy(c, i):
+        first, last = chunks[c]
+        span = pl.ds(first, last - first)
+        block = full_ref.at[core, ((x + 4 - i // 4) % 4) * 4 + (y + 4 - i % 4) % 4, span]
+        return copy(block, block, s_f.at[c, i], r_f.at[c, i], partner)
+
+    def after_core(j):
+        core_sum(j)
+        done = 2 * j + 2 if j < 4 else 9
+        for c, (first, last) in enumerate(chunks):
+            if last == done:
+                each(1, 16, lambda i: xy_copy(c, i).start())
 
     biases = [None] * 4
     for layer in range(3, -1, -1):
         local = (up * pre_ref[layer]).astype(bf16)
         wg = jnp.dot(actt_ref[layer], local, preferred_element_type=f32)
         for half in range(2):
-            part_ref[:, :, 2 * layer + half] = wg[:, half * 128 : half * 128 + 128].reshape(2, 16, 8, 128)
-        core_copy(layer).start()
+            part_ref[:, :, 2 * (3 - layer) + half] = wg[:, half * 128 : half * 128 + 128].reshape(2, 16, 8, 128)
+        core_copy(3 - layer).start()
         biases[layer] = jnp.sum(local.astype(f32), 0, keepdims=True)
         if layer > 0:
             up = nt_dot(local, w_ref[layer])
+        if layer < 3:
+            after_core(2 - layer)
     ext8 = jnp.where(
         row8 == 0,
         head[16:17],
@@ -325,51 +363,37 @@
         cols = ext[:, half * 128 : half * 128 + 128].reshape(3, 8, 128)
         part_ref[half, :, 8] = jnp.concatenate([cols, jnp.zeros((13, 8, 128), f32)], 0)
     core_copy(4).start()
-    for j in (3, 2, 1, 0, 4):
-        core_copy(j).wait()
-    part_ref[core] = part_ref[core] + core_in[...]
-
-    def xy_copy(i):
-        target = ((x + i // 4) % 4) * 4 + (y + i % 4) % 4
-        return copy(part_ref.at[core, target], xy_in.at[i], s_xy.at[i], r_xy.at[i], plane(i))
-
-    each(1, 16, lambda i: xy_copy(i).start())
-    each(1, 16, lambda i: xy_copy(i).wait())
-    total = part_ref[core, here]
-    for i in range(1, 16):
-        total = total + xy_in[i]
-    zsum_ref[z] = total
-
-    def z_copy(i):
-        return copy(zsum_ref.at[z], zsum_ref.at[z], s_z.at[i], r_z.at[i], ring(i))
-
-    each(1, 8, lambda i: z_copy(i).start())
-    each(1, 8, lambda i: z_copy(i).wait())
-    total = zsum_ref[0]
-    for i in range(1, 8):
-        total = total + zsum_ref[i]
-    full_ref[core, here] = total
-
-    def g_copy(i):
-        return copy(full_ref.at[core, here], full_ref.at[core, here], s_g.at[i], r_g.at[i], plane(i))
-
-    def f_copy(i):
-        block = ((x + 4 - i // 4) % 4) * 4 + (y + 4 - i % 4) % 4
-        return copy(full_ref.at[core, block], full_ref.at[core, block], s_f.at[i], r_f.at[i], partner)
-
-    each(1, 16, lambda i: g_copy(i).start())
-    f_copy(0).start()
-
-    def forward_on(i):
-        g_copy(i).wait_recv()
-        f_copy(i).start()
-
-    each(1, 16, forward_on)
-    each(1, 16, lambda i: g_copy(i).wait_send())
-    each(0, 16, lambda i: f_copy(i).wait())
+    after_core(3)
+    after_core(4)
+
+    for c, (first, last) in enumerate(chunks):
+        each(1, 16, lambda i: xy_copy(c, i).wait())
+        total = part_ref[core, here, first:last]
+        for i in range(1, 16):
+            total = total + xy_in[i, first:last]
+        zsum_ref[z, first:last] = total
+        each(1, 8, lambda i: z_copy(c, i).start())
+    for c, (first, last) in enumerate(chunks):
+        each(1, 8, lambda i: z_copy(c, i).wait())
+        total = zsum_ref[0, first:last]
+        for i in range(1, 8):
+            total = total + zsum_ref[i, first:last]
+        full_ref[core, here, first:last] = total
+        each(1, 16, lambda i: g_copy(c, i).start())
+        f_copy(c, 0).start()
+    for c in range(len(chunks)):
+
+        def forward_on(i):
+            g_copy(c, i).wait_recv()
+            f_copy(c, i).start()
+
+        each(1, 16, forward_on)
+    for c in range(len(chunks)):
+        each(1, 16, lambda i: g_copy(c, i).wait_send())
+        each(0, 16, lambda i: f_copy(c, i).wait())
     for layer in range(4):
         for half in range(2):
-            gw_ref[layer, :, half * 128 : half * 128 + 128] = full_ref[:, :, 2 * layer + half].reshape(256, 128)
+            gw_ref[layer, :, half * 128 : half * 128 + 128] = full_ref[:, :, 2 * (3 - layer) + half].reshape(256, 128)
     gc_ref[...] = jnp.concatenate(
         [full_ref[half, 0:2, 8].reshape(16, 128) for half in range(2)], 1
     )
@@ -437,9 +461,9 @@
             pltpu.VMEM((2, 16, 9, 8, 128), f32),
             dma((16,)), dma((16,)), dma((16,)), dma((16,)),
             dma((16,)), dma((16,)), dma((16,)), dma((16,)),
-            dma((5,)), dma((5,)), dma((16,)), dma((16,)),
-            dma((8,)), dma((8,)), dma((16,)), dma((16,)),
-            dma((16,)), dma((16,)),
+            dma((5,)), dma((5,)), dma((len(chunks), 16)), dma((len(chunks), 16)),
+            dma((len(chunks), 8)), dma((len(chunks), 8)), dma((len(chunks), 16)), dma((len(chunks), 16)),
+            dma((len(chunks), 16)), dma((len(chunks), 16)),
         ],
         compiler_params=pltpu.CompilerParams(
             collective_id=0, has_side_effects=True, vmem_limit_bytes=48 << 20

time: 67.9 us -> 62.1 us (0.915)
  Pallas kernels: 67.2 us -> 61.3 us
    pallas_call x1, Pallas kernels: 65.5 us -> 59.6 us  [on_device(): pl.pallas_call(kernel, name='condense', out_shape=results, in_specs=[hbm]...]
where the time goes in v3:
time: 62.1 us; the launch traced here: 61.9 us
  Pallas kernels  61.3 us (99%)
  between operations  0.64 us (1%)
    pallas_call x1, Pallas kernels, on_device(): pl.pallas_call(kernel, name='condense', out_shape=results, in_specs=[hbm]...  59.6 us
    pallas_call x1, Pallas kernels, on_device(): pl.pallas_call(deliver, name='deliver', out_shape=results, in_specs=[vmem...  1.65 us

profile of v3, /device:TPU:1, one launch (start us, length us, event | category | flops | bytes accessed | tf_op | source)
XLA Modules:
  0.0 61.9 jit_solution(3250998783581118939)
XLA Ops:
  0.6 59.6 %condense.1 = (f32[4,256,256]{2,1,0:T(8,128)S(1)}, f32[4,256]{1,0:T(4,128)S(1)}, f32[16,256]{1,0:T(8,128)S(1)}, f32[1,256]{1,0:T(1,128)S(1)}, f32[1,1]{1,0:T(1,128)}) custom-call(bf16[256,256]{1,0:T(8,128)(2,1)} %feat_hbm.1, bf16[4,256,256]{2,1,0:T(8,128)(2,1)} %w_hbm.1, f32[4,256]{1,0:T(4,128)} %b_hbm.1, bf16[16,256]{1,0:T(8,128)(2,1)} %wc_hbm.1, ...), custom_call_target="tpu_custom_call" | custom-call | tf_op jit(solution)/shard_map/condense/pallas_call | solution.py:426
  60.3 1.7 %deliver.1 = (f32[4,256,256]{2,1,0:T(8,128)}, f32[4,256]{1,0:T(4,128)}, f32[16,256]{1,0:T(8,128)}, f32[1,256]{1,0:T(1,128)}, f32[1,1]{1,0:T(1,128)}) custom-call(f32[4,256,256]{2,1,0:T(8,128)S(1)} %get-tuple-element.15.refs_0_, f32[4,256]{1,0:T(4,128)S(1)} %get-tuple-element.16.refs_1_, f32[16,256]{1,0:T(8,128)S(1)} %get-tuple-element.17.refs_2_, ...), custom_call_target="tpu_custom_call" | custom-call | tf_op jit(solution)/shard_map/deliver/pallas_call | solution.py:472

commit v4 on v3

--- a/solution.py
+++ b/solution.py
@@ -154,7 +154,9 @@
     lane8 = lanes_of((8, 256))
     pack = jnp.where(row8 == 0, charge, jnp.where(row8 == 1, key, jnp.where(row8 == 2, square, 0.0)))
     mine = jnp.concatenate([coords, pack], 0)
-    hits_ref[0] = mine
+    r8s = rows_of((8, 128))
+    tail_h = jnp.where(r8s == 0, charge[:, 0:128], jnp.where(r8s == 1, charge[:, 128:256], jnp.where(r8s == 2, key[:, 0:128], jnp.where(r8s == 3, key[:, 128:256], 0.0))))
+    hits_ref[0] = jnp.concatenate([coords[:, 0:128], coords[:, 128:256], tail_h], 0)
     sel = jnp.zeros((8, 256), f32)
     for k in range(8):
         sel = jnp.where((row8 == k) & (lane8 == hit_ref[k]), 1.0, sel)
@@ -208,44 +210,70 @@
     def hb_copy(i):
         return copy(hits_out.at[i], hits_back.at[i], s_hb.at[i], r_hb.at[i], plane_back(i))
 
-    def pairs(i):
-        @pl.when(i > 0)
-        def _():
-            hit_copy(i).wait()
-
-        blk = hits_ref[i]
-        xs = blk[0:16]
-        q = blk[16:17]
-        key_i = blk[17:18]
+    wide = 4
+    span = wide * 256
+    r16 = rows_of((16, span))
+
+    def over_hits(v):
+        return v if wide == 1 else jnp.concatenate([v] * wide, 1)
+
+    def pairs(j):
+        first = j * wide
+        for k in range(wide):
+            if k > 0:
+                hit_copy(first + k).wait()
+            else:
+
+                @pl.when(j > 0)
+                def _():
+                    hit_copy(first).wait()
+
+        blks = [hits_ref[first + k] for k in range(wide)]
+        xs = jnp.concatenate([v for b in blks for v in (b[0:16], b[16:32])], 1)
+        q = jnp.concatenate([v for b in blks for v in (b[32:33], b[33:34])], 1)
+        key_i = jnp.concatenate([v for b in blks for v in (b[34:35], b[35:36])], 1)
         xh, xm, xl = split3(xs)
-        sh, sm, sl = split3(blk[18:19])
-        r16 = rows_of((16, 256))
+        sh, sm, sl = split3(jnp.sum(xs * xs, 0, keepdims=True))
         tail_x = jnp.where(r16 == 0, sh, jnp.where(r16 == 1, sm, jnp.where(r16 == 2, sl, jnp.where(r16 < 6, 1.0, 0.0))))
-        xcat = jnp.concatenate([xh, xm, xh, xm, xl, xh, tail_x, jnp.zeros((16, 256), f32)], 0).astype(bf16)
+        xcat = jnp.concatenate([xh, xm, xh, xm, xl, xh, tail_x, jnp.zeros((16, span), f32)], 0).astype(bf16)
         d2 = jnp.maximum(jnp.dot(ycat_ref[...], xcat, preferred_element_type=f32), 0.0)
         t = d2 + dist_eps
         inv = lax.rsqrt(t)
         reach = jnp.maximum(1.0 - t * inv, 0.0)
-        match = id_ref[...] == key_i
+        match = over_hits(id_ref[...]) == key_i
         pot = jnp.where(match, d2, reach * reach)
         cc = jnp.where(match, 1.0, -(reach * inv))
-        pot_rows = jnp.sum(pot * qp_ref[...], 0, keepdims=True)
-        pot_ref[...] += pot * q
+        pot_rows = jnp.sum(pot * over_hits(qp_ref[...]), 0, keepdims=True)
+        weighted = pot * q
+        pot_sum = weighted[:, 0:256]
+        for k in range(1, wide):
+            pot_sum = pot_sum + weighted[:, 256 * k : 256 * k + 256]
+        pot_ref[...] += pot_sum
         cc_hi = cc.astype(bf16)
         cc_lo = (cc - cc_hi.astype(f32)).astype(bf16)
         ht = jnp.dot(yqt_ref[...], jnp.concatenate([cc_hi, cc_lo], 0), preferred_element_type=f32)
         ht = (ht[0:32] + ht[32:64]) + ht[64:96]
-        hits_out[i] = jnp.concatenate([ht[0:16], jnp.where(row8 == 1, pot_rows, ht[16:24])], 0)
+        for k in range(wide):
+            lo = slice(256 * k, 256 * k + 128)
+            hi = slice(256 * k + 128, 256 * k + 256)
+            ends = jnp.where(
+                r8s == 0, ht[16:17, lo], jnp.where(r8s == 1, ht[16:17, hi], jnp.where(r8s == 2, pot_rows[:, lo], pot_rows[:, hi]))
+            )
+            hits_out[first + k] = jnp.concatenate([ht[0:16, lo], ht[0:16, hi], ends], 0)
         xq = jnp.concatenate([xs * q, jnp.where(r16 == 0, q, 0.0)], 0)
         xqh, xqm, xql = split3(xq)
-        xq_all = jnp.concatenate([xqh, xqm, xql, jnp.zeros((32, 256), f32)], 0).astype(bf16)
+        xq_all = jnp.concatenate([xqh, xqm, xql, jnp.zeros((32, span), f32)], 0).astype(bf16)
         ptacc_ref[...] += nt_dot(cc_hi, xq_all) + nt_dot(cc_lo, xq_all)
-
-        @pl.when(i > 0)
-        def _():
-            hb_copy(i).start()
-
-    each(0, 16, pairs)
+        for k in range(wide):
+            if k > 0:
+                hb_copy(first + k).start()
+            else:
+
+                @pl.when(j > 0)
+                def _():
+                    hb_copy(first).start()
+
+    each(0, 16 // wide, pairs)
 
     acc = ptacc_ref[...]
     acc = (acc + pltpu.roll(acc, 96, 1)) + pltpu.roll(acc, 64, 1)
@@ -260,8 +288,10 @@
     hsum = hits_out[0]
     for i in range(1, 16):
         hsum = hsum + hits_back[i]
-    pot_i = hsum[17:18]
-    coord_grad = (2.0 * charge / HITS) * (coords * hsum[16:17] - hsum[0:16])
+    pull = jnp.concatenate([hsum[0:16], hsum[16:32]], 1)
+    coef_i = jnp.concatenate([hsum[32:33], hsum[33:34]], 1)
+    pot_i = jnp.concatenate([hsum[34:35], hsum[35:36]], 1)
+    coord_grad = (2.0 * charge / HITS) * (coords * coef_i - pull)
     each(1, 16, lambda i: pb_copy(i).wait())
     psum = pts_out[0]
     for i in range(1, 16):
@@ -442,9 +472,9 @@
             pltpu.VMEM((4, 256, 256), f32),
             pltpu.VMEM((4, 256, 256), bf16),
             pltpu.VMEM((4, 256, 256), bf16),
-            pltpu.VMEM((16, 24, 256), f32),
-            pltpu.VMEM((16, 24, 256), f32),
-            pltpu.VMEM((16, 24, 256), f32),
+            pltpu.VMEM((16, 40, 128), f32),
+            pltpu.VMEM((16, 40, 128), f32),
+            pltpu.VMEM((16, 40, 128), f32),
             pltpu.VMEM((16, 8, 128), f32),
             pltpu.VMEM((16, 8, 128), f32),
             pltpu.VMEM((16, 8, 128), f32),

time: 62.1 us -> 59.8 us (0.963)
  Pallas kernels: 61.3 us -> 59 us
    pallas_call x1, Pallas kernels: 59.6 us -> 57.4 us  [on_device(): pl.pallas_call(kernel, name='condense', out_shape=results, in_specs=[hbm]...]
where the time goes in v4:
time: 59.8 us; the launch traced here: 59.7 us
  Pallas kernels  59 us (99%)
  between operations  0.64 us (1%)
    pallas_call x1, Pallas kernels, on_device(): pl.pallas_call(kernel, name='condense', out_shape=results, in_specs=[hbm]...  57.4 us
    pallas_call x1, Pallas kernels, on_device(): pl.pallas_call(deliver, name='deliver', out_shape=results, in_specs=[vmem...  1.65 us

profile of v4, /device:TPU:1, one launch (start us, length us, event | category | flops | bytes accessed | tf_op | source)
XLA Modules:
  0.0 59.7 jit_solution(9435799799044456853)
XLA Ops:
  0.6 57.4 %condense.1 = (f32[4,256,256]{2,1,0:T(8,128)S(1)}, f32[4,256]{1,0:T(4,128)S(1)}, f32[16,256]{1,0:T(8,128)S(1)}, f32[1,256]{1,0:T(1,128)S(1)}, f32[1,1]{1,0:T(1,128)}) custom-call(bf16[256,256]{1,0:T(8,128)(2,1)} %feat_hbm.1, bf16[4,256,256]{2,1,0:T(8,128)(2,1)} %w_hbm.1, f32[4,256]{1,0:T(4,128)} %b_hbm.1, bf16[16,256]{1,0:T(8,128)(2,1)} %wc_hbm.1, ...), custom_call_target="tpu_custom_call" | custom-call | tf_op jit(solution)/shard_map/condense/pallas_call | solution.py:456
  58.0 1.7 %deliver.1 = (f32[4,256,256]{2,1,0:T(8,128)}, f32[4,256]{1,0:T(4,128)}, f32[16,256]{1,0:T(8,128)}, f32[1,256]{1,0:T(1,128)}, f32[1,1]{1,0:T(1,128)}) custom-call(f32[4,256,256]{2,1,0:T(8,128)S(1)} %get-tuple-element.15.refs_0_, f32[4,256]{1,0:T(4,128)S(1)} %get-tuple-element.16.refs_1_, f32[16,256]{1,0:T(8,128)S(1)} %get-tuple-element.17.refs_2_, ...), custom_call_target="tpu_custom_call" | custom-call | tf_op jit(solution)/shard_map/deliver/pallas_call | solution.py:502

commit v5 on v4

--- a/solution.py
+++ b/solution.py
@@ -12,7 +12,8 @@
 MESH = pl.DeviceIdType.MESH
 HITS = 65536.0
 POINTS = 2048.0
-chunks = ((0, 4), (4, 9))
+chunks = ((0, 4), (4, 6))
+zchunks = ((0, 4), (4, 5))
 
 
 def split3(v):
@@ -47,8 +48,10 @@
     hits_ref, hits_back, hits_out, pts_ref, pts_back, pts_out,
     ycat_ref, yqt_ref, qp_ref, id_ref, pot_ref, ptacc_ref,
     part_ref, core_in, xy_in, zsum_ref, full_ref,
+    partz_ref, corez_in, z_in, xysum_ref, fullz_ref,
     s_hit, r_hit, s_pt, r_pt, s_hb, r_hb, s_pb, r_pb,
     s_core, r_core, s_xy, r_xy, s_z, r_z, s_g, r_g, s_f, r_f,
+    s_bz, r_bz, s_bx, r_bx, s_bg, r_bg, s_bf, r_bf,
 ):
     loads = [
         pltpu.make_async_copy(src, dst, s_in.at[i])
@@ -104,6 +107,10 @@
             src_ref=src, dst_ref=dst, send_sem=ssem, recv_sem=rsem,
             device_id=target, device_id_type=MESH,
         )
+
+    def settle(ref, *sems):
+        for sem in sems:
+            pltpu.make_async_copy(ref, ref, sem).wait()
 
     def each(first, last, body):
         def step(i, carry):
@@ -172,10 +179,10 @@
     pl.semaphore_wait(barrier, 30)
 
     def pt_copy(i):
-        return copy(pts_ref.at[0], pts_ref.at[i], s_pt.at[i], r_pt.at[i], column(i))
+        return copy(pts_ref.at[0], pts_ref.at[i], s_pt.at[0], r_pt.at[0], column(i))
 
     def hit_copy(i):
-        return copy(hits_ref.at[0], hits_ref.at[i], s_hit.at[i], r_hit.at[i], plane(i))
+        return copy(hits_ref.at[0], hits_ref.at[i], s_hit.at[0], r_hit.at[i // 4], plane(i))
 
     each(1, 16, lambda i: pt_copy(i).start())
     each(1, 16, lambda i: hit_copy(i).start())
@@ -190,7 +197,7 @@
     ptacc_ref[...] = jnp.zeros((128, 128), f32)
     pot_ref[...] = jnp.zeros((128, 256), f32)
 
-    each(1, 16, lambda i: pt_copy(i).wait())
+    settle(pts_ref.at[pl.ds(1, 15)], s_pt.at[0], r_pt.at[0])
     points = pts_ref[...].reshape(128, 128)
     qp_ref[...] = jnp.broadcast_to(points[:, 16:17], (128, 256))
     id_ref[...] = jnp.broadcast_to(points[:, 17:18], (128, 256))
@@ -208,7 +215,7 @@
     yqt_ref[...] = jnp.concatenate([yqt, yqt], 1)
 
     def hb_copy(i):
-        return copy(hits_out.at[i], hits_back.at[i], s_hb.at[i], r_hb.at[i], plane_back(i))
+        return copy(hits_out.at[i], hits_back.at[i], s_hb.at[0], r_hb.at[0], plane_back(i))
 
     wide = 4
     span = wide * 256
@@ -219,14 +226,13 @@
 
     def pairs(j):
         first = j * wide
-        for k in range(wide):
-            if k > 0:
-                hit_copy(first + k).wait()
-            else:
-
-                @pl.when(j > 0)
-                def _():
-                    hit_copy(first).wait()
+        @pl.when(j == 0)
+        def _():
+            settle(hits_ref.at[pl.ds(1, wide - 1)], r_hit.at[0])
+
+        @pl.when(j > 0)
+        def _():
+            settle(hits_ref.at[pl.ds(first, wide)], r_hit.at[j])
 
         blks = [hits_ref[first + k] for k in range(wide)]
         xs = jnp.concatenate([v for b in blks for v in (b[0:16], b[16:32])], 1)
@@ -274,6 +280,7 @@
                     hb_copy(first).start()
 
     each(0, 16 // wide, pairs)
+    settle(hits_ref.at[pl.ds(1, 15)], s_hit.at[0])
 
     acc = ptacc_ref[...]
     acc = (acc + pltpu.roll(acc, 96, 1)) + pltpu.roll(acc, 64, 1)
@@ -281,10 +288,10 @@
     pts_out[...] = jnp.where(lanes_of((128, 128)) == 17, pot_cols, acc).reshape(16, 8, 128)
 
     def pb_copy(i):
-        return copy(pts_out.at[i], pts_back.at[i], s_pb.at[i], r_pb.at[i], column_back(i))
+        return copy(pts_out.at[i], pts_back.at[i], s_pb.at[0], r_pb.at[0], column_back(i))
 
     each(1, 16, lambda i: pb_copy(i).start())
-    each(1, 16, lambda i: hb_copy(i).wait())
+    settle(hits_back.at[pl.ds(1, 15)], s_hb.at[0], r_hb.at[0])
     hsum = hits_out[0]
     for i in range(1, 16):
         hsum = hsum + hits_back[i]
@@ -292,7 +299,7 @@
     coef_i = jnp.concatenate([hsum[32:33], hsum[33:34]], 1)
     pot_i = jnp.concatenate([hsum[34:35], hsum[35:36]], 1)
     coord_grad = (2.0 * charge / HITS) * (coords * coef_i - pull)
-    each(1, 16, lambda i: pb_copy(i).wait())
+    settle(pts_back.at[pl.ds(1, 15)], s_pb.at[0], r_pb.at[0])
     psum = pts_out[0]
     for i in range(1, 16):
         psum = psum + pts_back[i]
@@ -320,61 +327,79 @@
     up = tn_dot(low, wcb)
 
     def core_copy(j):
-        first, count = (2 * j, 2) if j < 4 else (8, 1)
-        return copy(
-            part_ref.at[other, :, pl.ds(first, count)], core_in.at[:, pl.ds(first, count)],
-            s_core.at[j], r_core.at[j], partner,
-        )
+        if j == 0 or j == 4:
+            span = pl.ds(0, 4) if j == 0 else pl.ds(4, 1)
+            src, dst = partz_ref.at[other, :, span], corez_in.at[:, span]
+        else:
+            span = pl.ds(2 * j - 2, 2)
+            src, dst = part_ref.at[other, :, span], core_in.at[:, span]
+        return copy(src, dst, s_core.at[j], r_core.at[j], partner)
 
     def core_sum(j):
         core_copy(j).wait()
-        first, count = (2 * j, 2) if j < 4 else (8, 1)
-        part_ref[core, :, first : first + count] += core_in[:, first : first + count]
+        if j == 0 or j == 4:
+            first, last = (0, 4) if j == 0 else (4, 5)
+            partz_ref[core, :, first:last] += corez_in[:, first:last]
+        else:
+            part_ref[core, :, 2 * j - 2 : 2 * j] += core_in[:, 2 * j - 2 : 2 * j]
+
+    def span_of(c, table):
+        first, last = table[c]
+        return pl.ds(first, last - first)
 
     def xy_copy(c, i):
-        first, last = chunks[c]
-        span = pl.ds(first, last - first)
+        span = span_of(c, chunks)
         target = ((x + i // 4) % 4) * 4 + (y + i % 4) % 4
-        return copy(
-            part_ref.at[core, target, span], xy_in.at[i, span], s_xy.at[c, i], r_xy.at[c, i], plane(i)
-        )
+        return copy(part_ref.at[core, target, span], xy_in.at[i, span], s_xy.at[c], r_xy.at[c], plane(i))
 
     def z_copy(c, i):
-        first, last = chunks[c]
-        span = pl.ds(first, last - first)
-        return copy(zsum_ref.at[z, span], zsum_ref.at[z, span], s_z.at[c, i], r_z.at[c, i], ring(i))
+        block = zsum_ref.at[z, span_of(c, chunks)]
+        return copy(block, block, s_z.at[c], r_z.at[c], ring(i))
 
     def g_copy(c, i):
-        first, last = chunks[c]
-        span = pl.ds(first, last - first)
-        block = full_ref.at[core, here, span]
-        return copy(block, block, s_g.at[c, i], r_g.at[c, i], plane(i))
+        block = full_ref.at[core, here, span_of(c, chunks)]
+        return copy(block, block, s_g.at[c], r_g.at[c, i // 4], plane(i))
 
     def f_copy(c, i):
-        first, last = chunks[c]
-        span = pl.ds(first, last - first)
-        block = full_ref.at[core, ((x + 4 - i // 4) % 4) * 4 + (y + 4 - i % 4) % 4, span]
-        return copy(block, block, s_f.at[c, i], r_f.at[c, i], partner)
-
-    def after_core(j):
-        core_sum(j)
-        done = 2 * j + 2 if j < 4 else 9
-        for c, (first, last) in enumerate(chunks):
-            if last == done:
-                each(1, 16, lambda i: xy_copy(c, i).start())
-
-    biases = [None] * 4
-    for layer in range(3, -1, -1):
+        block = full_ref.at[core, pl.ds(((x + 4 - i) % 4) * 4, 4), span_of(c, chunks)]
+        return copy(block, block, s_f.at[c], r_f.at[c], partner)
+
+    def bz_copy(c, i):
+        span = span_of(c, zchunks)
+        return copy(partz_ref.at[core, (z + i) % 8, span], z_in.at[i, span], s_bz.at[c], r_bz.at[c], ring(i))
+
+    def bx_copy(c, i):
+        block = xysum_ref.at[here, span_of(c, zchunks)]
+        return copy(block, block, s_bx.at[c], r_bx.at[c], plane(i))
+
+    def bg_copy(c, i):
+        block = fullz_ref.at[core, z, span_of(c, zchunks)]
+        return copy(block, block, s_bg.at[c], r_bg.at[c], ring(i))
+
+    def bf_copy(c):
+        block = fullz_ref.at[core, :, span_of(c, zchunks)]
+        return copy(block, block, s_bf.at[c], r_bf.at[c], partner)
+
+    def layer_grad(layer, up):
         local = (up * pre_ref[layer]).astype(bf16)
         wg = jnp.dot(actt_ref[layer], local, preferred_element_type=f32)
         for half in range(2):
-            part_ref[:, :, 2 * (3 - layer) + half] = wg[:, half * 128 : half * 128 + 128].reshape(2, 16, 8, 128)
+            cols = wg[:, half * 128 : half * 128 + 128]
+            if layer == 3:
+                partz_ref[:, :, 2 * half : 2 * half + 2] = cols.reshape(2, 8, 2, 8, 128)
+            else:
+                part_ref[:, :, 2 * (2 - layer) + half] = cols.reshape(2, 16, 8, 128)
         core_copy(3 - layer).start()
-        biases[layer] = jnp.sum(local.astype(f32), 0, keepdims=True)
-        if layer > 0:
-            up = nt_dot(local, w_ref[layer])
-        if layer < 3:
-            after_core(2 - layer)
+        bias = jnp.sum(local.astype(f32), 0, keepdims=True)
+        return bias, nt_dot(local, w_ref[layer]) if layer > 0 else None
+
+    biases = [None] * 4
+    biases[3], up = layer_grad(3, up)
+    biases[2], up = layer_grad(2, up)
+    biases[1], up = layer_grad(1, up)
+    biases[0], up = layer_grad(0, up)
+    core_sum(0)
+    each(1, 8, lambda i: bz_copy(0, i).start())
     ext8 = jnp.where(
         row8 == 0,
         head[16:17],
@@ -391,46 +416,103 @@
     ext = jnp.concatenate([head[0:16], ext8], 0)
     for half in range(2):
         cols = ext[:, half * 128 : half * 128 + 128].reshape(3, 8, 128)
-        part_ref[half, :, 8] = jnp.concatenate([cols, jnp.zeros((13, 8, 128), f32)], 0)
+        partz_ref[half, :, 4] = jnp.concatenate([cols, jnp.zeros((5, 8, 128), f32)], 0)
     core_copy(4).start()
-    after_core(3)
-    after_core(4)
-
-    for c, (first, last) in enumerate(chunks):
-        each(1, 16, lambda i: xy_copy(c, i).wait())
+    core_sum(1)
+    core_sum(2)
+    each(1, 16, lambda i: xy_copy(0, i).start())
+    core_sum(3)
+    each(1, 16, lambda i: xy_copy(1, i).start())
+    core_sum(4)
+    each(1, 8, lambda i: bz_copy(1, i).start())
+
+    def z_first(c):
+        first, last = zchunks[c]
+        settle(z_in.at[pl.ds(1, 7), span_of(c, zchunks)], s_bz.at[c], r_bz.at[c])
+        total = partz_ref[core, z, first:last]
+        for i in range(1, 8):
+            total = total + z_in[i, first:last]
+        xysum_ref[here, first:last] = total
+        each(1, 16, lambda i: bx_copy(c, i).start())
+
+    def plane_first(c):
+        first, last = chunks[c]
+        settle(xy_in.at[pl.ds(1, 15), span_of(c, chunks)], s_xy.at[c], r_xy.at[c])
         total = part_ref[core, here, first:last]
         for i in range(1, 16):
             total = total + xy_in[i, first:last]
         zsum_ref[z, first:last] = total
         each(1, 8, lambda i: z_copy(c, i).start())
-    for c, (first, last) in enumerate(chunks):
-        each(1, 8, lambda i: z_copy(c, i).wait())
+
+    def z_last(c):
+        first, last = zchunks[c]
+        settle(xysum_ref.at[pl.ds(1, 15), span_of(c, zchunks)], s_bx.at[c], r_bx.at[c])
+        total = xysum_ref[0, first:last]
+        for i in range(1, 16):
+            total = total + xysum_ref[i, first:last]
+        fullz_ref[core, z, first:last] = total
+        each(1, 8, lambda i: bg_copy(c, i).start())
+
+    def plane_last(c):
+        first, last = chunks[c]
+        settle(zsum_ref.at[pl.ds(1, 7), span_of(c, chunks)], s_z.at[c], r_z.at[c])
         total = zsum_ref[0, first:last]
         for i in range(1, 8):
             total = total + zsum_ref[i, first:last]
         full_ref[core, here, first:last] = total
         each(1, 16, lambda i: g_copy(c, i).start())
+
+    z_first(0)
+    plane_first(0)
+    z_first(1)
+    plane_first(1)
+    z_last(0)
+    plane_last(0)
+    z_last(1)
+    plane_last(1)
+    def z_hand_on(c):
+        settle(fullz_ref.at[core, pl.ds(1, 7), span_of(c, zchunks)], s_bg.at[c], r_bg.at[c])
+        bf_copy(c).start()
+
+    def plane_hand_on(c):
+        span = span_of(c, chunks)
+        settle(full_ref.at[core, pl.ds(1, 3), span], r_g.at[c, 0])
         f_copy(c, 0).start()
-    for c in range(len(chunks)):
-
-        def forward_on(i):
-            g_copy(c, i).wait_recv()
+
+        def step(i):
+            settle(full_ref.at[core, pl.ds(0, 4), span], r_g.at[c, i])
             f_copy(c, i).start()
-
-        each(1, 16, forward_on)
-    for c in range(len(chunks)):
-        each(1, 16, lambda i: g_copy(c, i).wait_send())
-        each(0, 16, lambda i: f_copy(c, i).wait())
-    for layer in range(4):
+        each(1, 4, step)
+
+    def place(layer):
         for half in range(2):
-            gw_ref[layer, :, half * 128 : half * 128 + 128] = full_ref[:, :, 2 * (3 - layer) + half].reshape(256, 128)
+            cols = slice(half * 128, half * 128 + 128)
+            if layer == 3:
+                gw_ref[3, :, cols] = fullz_ref[:, :, 2 * half : 2 * half + 2].reshape(256, 128)
+            else:
+                gw_ref[layer, :, cols] = full_ref[:, :, 2 * (2 - layer) + half].reshape(256, 128)
+
+    z_hand_on(0)
+    z_hand_on(1)
+    plane_hand_on(0)
+    plane_hand_on(1)
+    bf_copy(0).wait()
+    place(3)
+    bf_copy(1).wait()
     gc_ref[...] = jnp.concatenate(
-        [full_ref[half, 0:2, 8].reshape(16, 128) for half in range(2)], 1
+        [fullz_ref[half, 0:2, 4].reshape(16, 128) for half in range(2)], 1
     )
-    last = jnp.concatenate([full_ref[half, 2, 8] for half in range(2)], 1)
+    last = jnp.concatenate([fullz_ref[half, 2, 4] for half in range(2)], 1)
     gbeta_ref[...] = last[0:1]
     gb_ref[...] = last[1:5]
     loss_ref[...] = last[5:6, 0:1]
+
+    for c in range(2):
+        settle(full_ref.at[core, pl.ds(1, 15), span_of(c, chunks)], s_g.at[c])
+        settle(full_ref.at[core, :, span_of(c, chunks)], s_f.at[c], r_f.at[c])
+    place(2)
+    place(1)
+    place(0)
 
 
 def deliver(*refs):
@@ -484,16 +566,23 @@
             pltpu.VMEM((128, 256), f32),
             pltpu.VMEM((128, 256), f32),
             pltpu.VMEM((128, 128), f32),
-            pltpu.VMEM((2, 16, 9, 8, 128), f32),
-            pltpu.VMEM((16, 9, 8, 128), f32),
-            pltpu.VMEM((16, 9, 8, 128), f32),
-            pltpu.VMEM((8, 9, 8, 128), f32),
-            pltpu.VMEM((2, 16, 9, 8, 128), f32),
-            dma((16,)), dma((16,)), dma((16,)), dma((16,)),
-            dma((16,)), dma((16,)), dma((16,)), dma((16,)),
-            dma((5,)), dma((5,)), dma((len(chunks), 16)), dma((len(chunks), 16)),
-            dma((len(chunks), 8)), dma((len(chunks), 8)), dma((len(chunks), 16)), dma((len(chunks), 16)),
-            dma((len(chunks), 16)), dma((len(chunks), 16)),
+            pltpu.VMEM((2, 16, 6, 8, 128), f32),
+            pltpu.VMEM((16, 6, 8, 128), f32),
+            pltpu.VMEM((16, 6, 8, 128), f32),
+            pltpu.VMEM((8, 6, 8, 128), f32),
+            pltpu.VMEM((2, 16, 6, 8, 128), f32),
+            pltpu.VMEM((2, 8, 5, 8, 128), f32),
+            pltpu.VMEM((8, 5, 8, 128), f32),
+            pltpu.VMEM((8, 5, 8, 128), f32),
+            pltpu.VMEM((16, 5, 8, 128), f32),
+            pltpu.VMEM((2, 8, 5, 8, 128), f32),
+            dma((1,)), dma((4,)), dma((1,)), dma((1,)),
+            dma((1,)), dma((1,)), dma((1,)), dma((1,)),
+            dma((5,)), dma((5,)), dma((2,)), dma((2,)),
+            dma((2,)), dma((2,)), dma((2,)), dma((2, 4)),
+            dma((2,)), dma((2,)),
+            dma((2,)), dma((2,)), dma((2,)), dma((2,)),
+            dma((2,)), dma((2,)), dma((2,)), dma((2,)),
         ],
         compiler_params=pltpu.CompilerParams(
             collective_id=0, has_side_effects=True, vmem_limit_bytes=48 << 20

time: 59.8 us -> 54.2 us (0.906)
  Pallas kernels: 59 us -> 53.5 us
    pallas_call x1, Pallas kernels: 57.4 us -> 51.8 us  [on_device(): pl.pallas_call(kernel, name='condense', out_shape=results, in_specs=[hbm]...]
where the time goes in v5:
time: 54.2 us; the launch traced here: 54.1 us
  Pallas kernels  53.5 us (99%)
  between operations  0.64 us (1%)
    pallas_call x1, Pallas kernels, on_device(): pl.pallas_call(kernel, name='condense', out_shape=results, in_specs=[hbm]...  51.8 us
    pallas_call x1, Pallas kernels, on_device(): pl.pallas_call(deliver, name='deliver', out_shape=results, in_specs=[vmem...  1.65 us

profile of v5, /device:TPU:1, one launch (start us, length us, event | category | flops | bytes accessed | tf_op | source)
XLA Modules:
  0.0 54.1 jit_solution(6607883042607356156)
XLA Ops:
  0.6 51.8 %condense.1 = (f32[4,256,256]{2,1,0:T(8,128)S(1)}, f32[4,256]{1,0:T(4,128)S(1)}, f32[16,256]{1,0:T(8,128)S(1)}, f32[1,256]{1,0:T(1,128)S(1)}, f32[1,1]{1,0:T(1,128)}) custom-call(bf16[256,256]{1,0:T(8,128)(2,1)} %feat_hbm.1, bf16[4,256,256]{2,1,0:T(8,128)(2,1)} %w_hbm.1, f32[4,256]{1,0:T(4,128)} %b_hbm.1, bf16[16,256]{1,0:T(8,128)(2,1)} %wc_hbm.1, ...), custom_call_target="tpu_custom_call" | custom-call | tf_op jit(solution)/shard_map/condense/pallas_call | solution.py:538
  52.5 1.7 %deliver.1 = (f32[4,256,256]{2,1,0:T(8,128)}, f32[4,256]{1,0:T(4,128)}, f32[16,256]{1,0:T(8,128)}, f32[1,256]{1,0:T(1,128)}, f32[1,1]{1,0:T(1,128)}) custom-call(f32[4,256,256]{2,1,0:T(8,128)S(1)} %get-tuple-element.15.refs_0_, f32[4,256]{1,0:T(4,128)S(1)} %get-tuple-element.16.refs_1_, f32[16,256]{1,0:T(8,128)S(1)} %get-tuple-element.17.refs_2_, ...), custom_call_target="tpu_custom_call" | custom-call | tf_op jit(solution)/shard_map/deliver/pallas_call | solution.py:591

commit v6 on v5

--- a/solution.py
+++ b/solution.py
@@ -12,7 +12,10 @@
 MESH = pl.DeviceIdType.MESH
 HITS = 65536.0
 POINTS = 2048.0
-chunks = ((0, 4), (4, 6))
+far_plane = (10, 6, 9, 11, 14, 2, 8, 5, 7, 13, 15, 1, 3, 4, 12)
+far_column = (9, 8, 7, 11, 6, 10, 5, 13, 4, 12, 3, 15, 2, 14, 1)
+far_ring = (4, 3, 5, 2, 6, 1, 7)
+chunks = ((0, 2), (2, 4), (4, 6))
 zchunks = ((0, 4), (4, 5))
 
 
@@ -117,6 +120,10 @@
             body(i)
             return carry
         lax.fori_loop(first, last, step, 0)
+
+    def over(order, body):
+        for i in order:
+            body(i)
 
     barrier = pltpu.get_barrier_semaphore()
 
@@ -184,8 +191,8 @@
     def hit_copy(i):
         return copy(hits_ref.at[0], hits_ref.at[i], s_hit.at[0], r_hit.at[i // 4], plane(i))
 
-    each(1, 16, lambda i: pt_copy(i).start())
-    each(1, 16, lambda i: hit_copy(i).start())
+    over(far_column, lambda i: pt_copy(i).start())
+    over(far_plane, lambda i: hit_copy(i).start())
 
     actt_ref[0] = feat_ref[...].T
     for layer in range(4):
@@ -224,7 +231,8 @@
     def over_hits(v):
         return v if wide == 1 else jnp.concatenate([v] * wide, 1)
 
-    def pairs(j):
+    def pairs(turn):
+        j = (turn * 2) % 4 + turn // 2
         first = j * wide
         @pl.when(j == 0)
         def _():
@@ -290,7 +298,7 @@
     def pb_copy(i):
         return copy(pts_out.at[i], pts_back.at[i], s_pb.at[0], r_pb.at[0], column_back(i))
 
-    each(1, 16, lambda i: pb_copy(i).start())
+    over(far_column, lambda i: pb_copy(i).start())
     settle(hits_back.at[pl.ds(1, 15)], s_hb.at[0], r_hb.at[0])
     hsum = hits_out[0]
     for i in range(1, 16):
@@ -399,7 +407,7 @@
     biases[1], up = layer_grad(1, up)
     biases[0], up = layer_grad(0, up)
     core_sum(0)
-    each(1, 8, lambda i: bz_copy(0, i).start())
+    over(far_ring, lambda i: bz_copy(0, i).start())
     ext8 = jnp.where(
         row8 == 0,
         head[16:17],
@@ -419,12 +427,13 @@
         partz_ref[half, :, 4] = jnp.concatenate([cols, jnp.zeros((5, 8, 128), f32)], 0)
     core_copy(4).start()
     core_sum(1)
+    over(far_plane, lambda i: xy_copy(0, i).start())
     core_sum(2)
-    each(1, 16, lambda i: xy_copy(0, i).start())
+    over(far_plane, lambda i: xy_copy(1, i).start())
     core_sum(3)
-    each(1, 16, lambda i: xy_copy(1, i).start())
+    over(far_plane, lambda i: xy_copy(2, i).start())
     core_sum(4)
-    each(1, 8, lambda i: bz_copy(1, i).start())
+    over(far_ring, lambda i: bz_copy(1, i).start())
 
     def z_first(c):
         first, last = zchunks[c]
@@ -433,7 +442,7 @@
         for i in range(1, 8):
             total = total + z_in[i, first:last]
         xysum_ref[here, first:last] = total
-        each(1, 16, lambda i: bx_copy(c, i).start())
+        over(far_plane, lambda i: bx_copy(c, i).start())
 
     def plane_first(c):
         first, last = chunks[c]
@@ -442,7 +451,7 @@
         for i in range(1, 16):
             total = total + xy_in[i, first:last]
         zsum_ref[z, first:last] = total
-        each(1, 8, lambda i: z_copy(c, i).start())
+        over(far_ring, lambda i: z_copy(c, i).start())
 
     def z_last(c):
         first, last = zchunks[c]
@@ -451,7 +460,7 @@
         for i in range(1, 16):
             total = total + xysum_ref[i, first:last]
         fullz_ref[core, z, first:last] = total
-        each(1, 8, lambda i: bg_copy(c, i).start())
+        over(far_ring, lambda i: bg_copy(c, i).start())
 
     def plane_last(c):
         first, last = chunks[c]
@@ -460,16 +469,19 @@
         for i in range(1, 8):
             total = total + zsum_ref[i, first:last]
         full_ref[core, here, first:last] = total
-        each(1, 16, lambda i: g_copy(c, i).start())
+        over(far_plane, lambda i: g_copy(c, i).start())
 
     z_first(0)
     plane_first(0)
+    plane_first(1)
     z_first(1)
-    plane_first(1)
+    plane_first(2)
     z_last(0)
     plane_last(0)
+    plane_last(1)
     z_last(1)
-    plane_last(1)
+    plane_last(2)
+
     def z_hand_on(c):
         settle(fullz_ref.at[core, pl.ds(1, 7), span_of(c, zchunks)], s_bg.at[c], r_bg.at[c])
         bf_copy(c).start()
@@ -492,10 +504,11 @@
             else:
                 gw_ref[layer, :, cols] = full_ref[:, :, 2 * (2 - layer) + half].reshape(256, 128)
 
+    plane_hand_on(0)
     z_hand_on(0)
     z_hand_on(1)
-    plane_hand_on(0)
     plane_hand_on(1)
+    plane_hand_on(2)
     bf_copy(0).wait()
     place(3)
     bf_copy(1).wait()
@@ -507,7 +520,7 @@
     gb_ref[...] = last[1:5]
     loss_ref[...] = last[5:6, 0:1]
 
-    for c in range(2):
+    for c in range(3):
         settle(full_ref.at[core, pl.ds(1, 15), span_of(c, chunks)], s_g.at[c])
         settle(full_ref.at[core, :, span_of(c, chunks)], s_f.at[c], r_f.at[c])
     place(2)
@@ -578,9 +591,9 @@
             pltpu.VMEM((2, 8, 5, 8, 128), f32),
             dma((1,)), dma((4,)), dma((1,)), dma((1,)),
             dma((1,)), dma((1,)), dma((1,)), dma((1,)),
-            dma((5,)), dma((5,)), dma((2,)), dma((2,)),
-            dma((2,)), dma((2,)), dma((2,)), dma((2, 4)),
-            dma((2,)), dma((2,)),
+            dma((5,)), dma((5,)), dma((3,)), dma((3,)),
+            dma((3,)), dma((3,)), dma((3,)), dma((3, 4)),
+            dma((3,)), dma((3,)),
             dma((2,)), dma((2,)), dma((2,)), dma((2,)),
             dma((2,)), dma((2,)), dma((2,)), dma((2,)),
         ],

time: 54.2 us -> 50.5 us (0.932)
  Pallas kernels: 53.5 us -> 49.8 us
    pallas_call x1, Pallas kernels: 51.8 us -> 48.1 us  [on_device(): pl.pallas_call(kernel, name='condense', out_shape=results, in_specs=[hbm]...]
where the time goes in v6:
time: 50.5 us; the launch traced here: 50.4 us
  Pallas kernels  49.8 us (99%)
  between operations  0.64 us (1%)
    pallas_call x1, Pallas kernels, on_device(): pl.pallas_call(kernel, name='condense', out_shape=results, in_specs=[hbm]...  48.1 us
    pallas_call x1, Pallas kernels, on_device(): pl.pallas_call(deliver, name='deliver', out_shape=results, in_specs=[vmem...  1.65 us

profile of v6, /device:TPU:1, one launch (start us, length us, event | category | flops | bytes accessed | tf_op | source)
XLA Modules:
  0.0 50.4 jit_solution(12903211079071430633)
XLA Ops:
  0.6 48.1 %condense.1 = (f32[4,256,256]{2,1,0:T(8,128)S(1)}, f32[4,256]{1,0:T(4,128)S(1)}, f32[16,256]{1,0:T(8,128)S(1)}, f32[1,256]{1,0:T(1,128)S(1)}, f32[1,1]{1,0:T(1,128)}) custom-call(bf16[256,256]{1,0:T(8,128)(2,1)} %feat_hbm.1, bf16[4,256,256]{2,1,0:T(8,128)(2,1)} %w_hbm.1, f32[4,256]{1,0:T(4,128)} %b_hbm.1, bf16[16,256]{1,0:T(8,128)(2,1)} %wc_hbm.1, ...), custom_call_target="tpu_custom_call" | custom-call | tf_op jit(solution)/shard_map/condense/pallas_call | solution.py:551
  48.8 1.7 %deliver.1 = (f32[4,256,256]{2,1,0:T(8,128)}, f32[4,256]{1,0:T(4,128)}, f32[16,256]{1,0:T(8,128)}, f32[1,256]{1,0:T(1,128)}, f32[1,1]{1,0:T(1,128)}) custom-call(f32[4,256,256]{2,1,0:T(8,128)S(1)} %get-tuple-element.15.refs_0_, f32[4,256]{1,0:T(4,128)S(1)} %get-tuple-element.16.refs_1_, f32[16,256]{1,0:T(8,128)S(1)} %get-tuple-element.17.refs_2_, ...), custom_call_target="tpu_custom_call" | custom-call | tf_op jit(solution)/shard_map/deliver/pallas_call | solution.py:604

commit v7 on v6

--- a/solution.py
+++ b/solution.py
@@ -74,8 +74,6 @@
             ]
         )
     ]
-    for load in loads:
-        load.start()
     lay = lax.axis_index("layer")
     phi = lax.axis_index("phi")
     z = (lay // 8) * 4 + phi % 4
@@ -127,10 +125,14 @@
 
     barrier = pltpu.get_barrier_semaphore()
 
-    def greet(i):
+    def greet(i, j):
+        pl.semaphore_signal(barrier, inc=1, device_id=column(j), device_id_type=MESH)
         pl.semaphore_signal(barrier, inc=1, device_id=plane(i), device_id_type=MESH)
-        pl.semaphore_signal(barrier, inc=1, device_id=column(i), device_id_type=MESH)
-    each(1, 16, greet)
+
+    for near, tall in zip(far_plane, far_column):
+        greet(near, tall)
+    for load in loads:
+        load.start()
 
     for load in loads[0:3]:
         load.wait()
@@ -278,7 +280,7 @@
         xqh, xqm, xql = split3(xq)
         xq_all = jnp.concatenate([xqh, xqm, xql, jnp.zeros((32, span), f32)], 0).astype(bf16)
         ptacc_ref[...] += nt_dot(cc_hi, xq_all) + nt_dot(cc_lo, xq_all)
-        for k in range(wide):
+        for k in (2, 1, 3, 0):
             if k > 0:
                 hb_copy(first + k).start()
             else:

time: 50.5 us -> 49.9 us (0.988)
  Pallas kernels: 49.8 us -> 49.1 us
    pallas_call x1, Pallas kernels: 48.1 us -> 47.5 us  [on_device(): pl.pallas_call(kernel, name='condense', out_shape=results, in_specs=[hbm]...]
where the time goes in v7:
time: 49.9 us; the launch traced here: 49.8 us
  Pallas kernels  49.1 us (98%)
  between operations  0.64 us (1%)
    pallas_call x1, Pallas kernels, on_device(): pl.pallas_call(kernel, name='condense', out_shape=results, in_specs=[hbm]...  47.5 us
    pallas_call x1, Pallas kernels, on_device(): pl.pallas_call(deliver, name='deliver', out_shape=results, in_specs=[vmem...  1.65 us

profile of v7, /device:TPU:1, one launch (start us, length us, event | category | flops | bytes accessed | tf_op | source)
XLA Modules:
  0.0 49.8 jit_solution(16868046642580375445)
XLA Ops:
  0.6 47.5 %condense.1 = (f32[4,256,256]{2,1,0:T(8,128)S(1)}, f32[4,256]{1,0:T(4,128)S(1)}, f32[16,256]{1,0:T(8,128)S(1)}, f32[1,256]{1,0:T(1,128)S(1)}, f32[1,1]{1,0:T(1,128)}) custom-call(bf16[256,256]{1,0:T(8,128)(2,1)} %feat_hbm.1, bf16[4,256,256]{2,1,0:T(8,128)(2,1)} %w_hbm.1, f32[4,256]{1,0:T(4,128)} %b_hbm.1, bf16[16,256]{1,0:T(8,128)(2,1)} %wc_hbm.1, ...), custom_call_target="tpu_custom_call" | custom-call | tf_op jit(solution)/shard_map/condense/pallas_call | solution.py:553
  48.1 1.7 %deliver.1 = (f32[4,256,256]{2,1,0:T(8,128)}, f32[4,256]{1,0:T(4,128)}, f32[16,256]{1,0:T(8,128)}, f32[1,256]{1,0:T(1,128)}, f32[1,1]{1,0:T(1,128)}) custom-call(f32[4,256,256]{2,1,0:T(8,128)S(1)} %get-tuple-element.15.refs_0_, f32[4,256]{1,0:T(4,128)S(1)} %get-tuple-element.16.refs_1_, f32[16,256]{1,0:T(8,128)S(1)} %get-tuple-element.17.refs_2_, ...), custom_call_target="tpu_custom_call" | custom-call | tf_op jit(solution)/shard_map/deliver/pallas_call | solution.py:606

commit v8 on v7

--- a/solution.py
+++ b/solution.py
@@ -14,6 +14,7 @@
 POINTS = 2048.0
 far_plane = (10, 6, 9, 11, 14, 2, 8, 5, 7, 13, 15, 1, 3, 4, 12)
 far_column = (9, 8, 7, 11, 6, 10, 5, 13, 4, 12, 3, 15, 2, 14, 1)
+far_hits = (10, 9, 11, 8, 2, 1, 3, 6, 5, 7, 4, 14, 13, 15, 12)
 far_ring = (4, 3, 5, 2, 6, 1, 7)
 chunks = ((0, 2), (2, 4), (4, 6))
 zchunks = ((0, 4), (4, 5))
@@ -194,7 +195,7 @@
         return copy(hits_ref.at[0], hits_ref.at[i], s_hit.at[0], r_hit.at[i // 4], plane(i))
 
     over(far_column, lambda i: pt_copy(i).start())
-    over(far_plane, lambda i: hit_copy(i).start())
+    over(far_hits, lambda i: hit_copy(i).start())
 
     actt_ref[0] = feat_ref[...].T
     for layer in range(4):
@@ -408,6 +409,8 @@
     biases[2], up = layer_grad(2, up)
     biases[1], up = layer_grad(1, up)
     biases[0], up = layer_grad(0, up)
+    core_sum(1)
+    over(far_plane, lambda i: xy_copy(0, i).start())
     core_sum(0)
     over(far_ring, lambda i: bz_copy(0, i).start())
     ext8 = jnp.where(
@@ -428,8 +431,6 @@
         cols = ext[:, half * 128 : half * 128 + 128].reshape(3, 8, 128)
         partz_ref[half, :, 4] = jnp.concatenate([cols, jnp.zeros((5, 8, 128), f32)], 0)
     core_copy(4).start()
-    core_sum(1)
-    over(far_plane, lambda i: xy_copy(0, i).start())
     core_sum(2)
     over(far_plane, lambda i: xy_copy(1, i).start())
     core_sum(3)
@@ -478,8 +479,8 @@
     plane_first(1)
     z_first(1)
     plane_first(2)
+    plane_last(0)
     z_last(0)
-    plane_last(0)
     plane_last(1)
     z_last(1)
     plane_last(2)
@@ -525,9 +526,7 @@
     for c in range(3):
         settle(full_ref.at[core, pl.ds(1, 15), span_of(c, chunks)], s_g.at[c])
         settle(full_ref.at[core, :, span_of(c, chunks)], s_f.at[c], r_f.at[c])
-    place(2)
-    place(1)
-    place(0)
+        place(2 - c)
 
 
 def deliver(*refs):

time: 49.9 us -> 49.7 us (level)
  no operation moved by 1% of the time
where the time goes in v8:
time: 49.7 us; the launch traced here: 49.6 us
  Pallas kernels  48.9 us (98%)
  between operations  0.64 us (1%)
    pallas_call x1, Pallas kernels, on_device(): pl.pallas_call(kernel, name='condense', out_shape=results, in_specs=[hbm]...  47.3 us
    pallas_call x1, Pallas kernels, on_device(): pl.pallas_call(deliver, name='deliver', out_shape=results, in_specs=[vmem...  1.65 us

profile of v8, /device:TPU:1, one launch (start us, length us, event | category | flops | bytes accessed | tf_op | source)
XLA Modules:
  0.0 49.6 jit_solution(7289318151031486854)
XLA Ops:
  0.6 47.3 %condense.1 = (f32[4,256,256]{2,1,0:T(8,128)S(1)}, f32[4,256]{1,0:T(4,128)S(1)}, f32[16,256]{1,0:T(8,128)S(1)}, f32[1,256]{1,0:T(1,128)S(1)}, f32[1,1]{1,0:T(1,128)}) custom-call(bf16[256,256]{1,0:T(8,128)(2,1)} %feat_hbm.1, bf16[4,256,256]{2,1,0:T(8,128)(2,1)} %w_hbm.1, f32[4,256]{1,0:T(4,128)} %b_hbm.1, bf16[16,256]{1,0:T(8,128)(2,1)} %wc_hbm.1, ...), custom_call_target="tpu_custom_call" | custom-call | tf_op jit(solution)/shard_map/condense/pallas_call | solution.py:552
  47.9 1.7 %deliver.1 = (f32[4,256,256]{2,1,0:T(8,128)}, f32[4,256]{1,0:T(4,128)}, f32[16,256]{1,0:T(8,128)}, f32[1,256]{1,0:T(1,128)}, f32[1,1]{1,0:T(1,128)}) custom-call(f32[4,256,256]{2,1,0:T(8,128)S(1)} %get-tuple-element.15.refs_0_, f32[4,256]{1,0:T(4,128)S(1)} %get-tuple-element.16.refs_1_, f32[16,256]{1,0:T(8,128)S(1)} %get-tuple-element.17.refs_2_, ...), custom_call_target="tpu_custom_call" | custom-call | tf_op jit(solution)/shard_map/deliver/pallas_call | solution.py:605

commit v9 on v8

--- a/solution.py
+++ b/solution.py
@@ -64,9 +64,7 @@
                 (feat_hbm, feat_ref),
                 (w_hbm.at[0], w_ref.at[0]),
                 (b_hbm, b_ref),
-                (w_hbm.at[1], w_ref.at[1]),
-                (w_hbm.at[2], w_ref.at[2]),
-                (w_hbm.at[3], w_ref.at[3]),
+                (w_hbm.at[pl.ds(1, 3)], w_ref.at[pl.ds(1, 3)]),
                 (wc_hbm, wc_ref),
                 (wb_hbm, wb_ref),
                 (track_hbm, track_ref),
@@ -139,13 +137,13 @@
         load.wait()
     hidden = feat_ref[...]
     for layer in range(4):
-        if layer > 0:
-            loads[2 + layer].wait()
+        if layer == 1:
+            loads[3].wait()
         pre = jnp.dot(hidden, w_ref[layer], preferred_element_type=f32) + b_ref[layer : layer + 1, :]
         pre_ref[layer] = pre
         hidden = (pre * jax.nn.sigmoid(pre)).astype(bf16)
         act_ref[layer] = hidden
-    for load in loads[6:11]:
+    for load in loads[4:9]:
         load.wait()
     wcb = jnp.concatenate(
         [
@@ -564,7 +562,7 @@
             pltpu.SMEM((8,), jnp.int32),
             pltpu.VMEM((256,), jnp.int32),
             pltpu.VMEM((256,), jnp.int32),
-            dma((11,)),
+            dma((9,)),
             pltpu.VMEM((4, 256, 256), f32),
             pltpu.VMEM((4, 256, 256), bf16),
             pltpu.VMEM((4, 256, 256), bf16),

time: 49.7 us -> 49.6 us (level)
  no operation moved by 1% of the time
where the time goes in v9:
time: 49.6 us; the launch traced here: 49.5 us
  Pallas kernels  48.9 us (99%)
  between operations  0.64 us (1%)
    pallas_call x1, Pallas kernels, on_device(): pl.pallas_call(kernel, name='condense', out_shape=results, in_specs=[hbm]...  47.2 us
    pallas_call x1, Pallas kernels, on_device(): pl.pallas_call(deliver, name='deliver', out_shape=results, in_specs=[vmem...  1.65 us

profile of v9, /device:TPU:1, one launch (start us, length us, event | category | flops | bytes accessed | tf_op | source)
XLA Modules:
  0.0 49.5 jit_solution(2852852257523782028)
XLA Ops:
  0.6 47.2 %condense.1 = (f32[4,256,256]{2,1,0:T(8,128)S(1)}, f32[4,256]{1,0:T(4,128)S(1)}, f32[16,256]{1,0:T(8,128)S(1)}, f32[1,256]{1,0:T(1,128)S(1)}, f32[1,1]{1,0:T(1,128)}) custom-call(bf16[256,256]{1,0:T(8,128)(2,1)} %feat_hbm.1, bf16[4,256,256]{2,1,0:T(8,128)(2,1)} %w_hbm.1, f32[4,256]{1,0:T(4,128)} %b_hbm.1, bf16[16,256]{1,0:T(8,128)(2,1)} %wc_hbm.1, ...), custom_call_target="tpu_custom_call" | custom-call | tf_op jit(solution)/shard_map/condense/pallas_call | solution.py:550
  47.9 1.7 %deliver.1 = (f32[4,256,256]{2,1,0:T(8,128)}, f32[4,256]{1,0:T(4,128)}, f32[16,256]{1,0:T(8,128)}, f32[1,256]{1,0:T(1,128)}, f32[1,1]{1,0:T(1,128)}) custom-call(f32[4,256,256]{2,1,0:T(8,128)S(1)} %get-tuple-element.15.refs_0_, f32[4,256]{1,0:T(4,128)S(1)} %get-tuple-element.16.refs_1_, f32[16,256]{1,0:T(8,128)S(1)} %get-tuple-element.17.refs_2_, ...), custom_call_target="tpu_custom_call" | custom-call | tf_op jit(solution)/shard_map/deliver/pallas_call | solution.py:603
